TPU v7x, 128 devices: a whole 4x4x4 slice. The times are simulated.
128 devices in a mesh: grp: 4 (over y_lo, core), blk: 32 (over z, x, y_hi).
Axes of the slice: x: 4, y: 4 (y_hi: 2, y_lo: 2; y = y_hi * 2 + y_lo), z: 4, core: 2. Of those that a mesh axis runs over, the one named last changes fastest.
Arguments:
- ratings: bfloat16 [8, 131072, 512], P(None, ('grp', 'blk')), may hold values from -6 to 6
- rated: int32 [8, 131072, 512], P(None, ('grp', 'blk')), may hold values 0 or 1
- user_factors: float32 [131072, 256], P(('grp', 'blk')), may hold values from -1.5 to 1.5
- item_ahead: bfloat16 [32768, 256], P(('grp', 'blk')), may hold values from -1.5 to 1.5
- item_behind: bfloat16 [32768, 256], P(('grp', 'blk')), may hold values from -1.5 to 1.5
- owners: int32 [2, 128], replicated, may hold values from 0 to 127, each once within a row
Outputs:
- user_out: float32 [131072, 256], P(('grp', 'blk'))
- ahead_out: bfloat16 [32768, 256], P(('grp', 'blk'))
- behind_out: bfloat16 [32768, 256], P(('grp', 'blk'))
Inputs may be any that keep to these rules, and one draw needn't show every extreme that they name: `owners`: each row is a permutation of 0 .. 127.
All inputs are finite; a program needn't handle non-finite values. No bound on the sum of `rated` on one device may be relied on, other than what follows from the above.
Results may differ from a plain program's by a relative error of at most 0.0086.
Values may be sent and summed in bfloat16 or wider, within the bound.
No kernel may reach another device: no remote copies, remote signals or barrier semaphores. Data moves between devices by JAX's collectives and lax.ppermute only.
A program may use at most 128 MiB of HBM per device.

v0:
```python
import jax
import jax.numpy as jnp
from jax import lax
from jax.sharding import PartitionSpec as P

RATE = 0.005
DECAY = 0.05


def sent_together(arrays, axis, dim, along):
    ends, at = ([], 0)
    for a in arrays[:-1]:
        at += a.shape[along]
        ends.append(at)
    both = jnp.concatenate(arrays, axis=along)
    return tuple(jnp.split(lax.all_gather(both, axis, axis=dim, tiled=True), ends, axis=along))


def sent_together_2(arrays, axis, split_dim, concat_dim, along):
    ends, at = ([], 0)
    for a in arrays[:-1]:
        at += a.shape[along]
        ends.append(at)
    both = jnp.concatenate(arrays, axis=along)
    return tuple(
        jnp.split(
            lax.all_to_all(both, axis, split_axis=split_dim, concat_axis=concat_dim, tiled=True),
            ends,
            axis=along,
        )
    )


def from_behind(array, axis, by):
    count = lax.axis_size(axis)
    return lax.ppermute(array, axis, [(i, (i + by) % count) for i in range(count)])


def body(ratings, rated, user_factors, item_ahead, item_behind, owners):
    half = item_ahead.shape[0]
    users = user_factors
    ahead = item_ahead
    behind = item_behind
    strata = ratings.shape[0]
    for stratum in range(strata):
        if stratum == strata // 2:
            row_count = lax.axis_size("blk")
            group_count = lax.axis_size("grp")
            group_self = lax.axis_index("grp")
            column_self = lax.axis_index("blk")
            targets = jnp.arange(group_count, dtype=jnp.int32) * row_count + column_self
            pieces = sent_together((ahead, behind), "blk", 0, 1)
            width = pieces[0].shape[0] // half
            source = group_self * row_count
            dest_a = lax.dynamic_slice_in_dim(owners[0], source, width)
            dest_b = lax.dynamic_slice_in_dim(owners[1], source, width)
            mask_a = (dest_a[:, None] == targets[None, :]).astype(jnp.bfloat16)
            mask_b = (dest_b[:, None] == targets[None, :]).astype(jnp.bfloat16)
            piece_a = pieces[0].reshape(width, half, -1)
            piece_b = pieces[1].reshape(width, half, -1)
            take_a = jnp.einsum("wg,whr->ghr", mask_a, piece_a, preferred_element_type=jnp.float32)
            take_b = jnp.einsum("wg,whr->ghr", mask_b, piece_b, preferred_element_type=jnp.float32)
            send_a = take_a.astype(jnp.bfloat16)
            send_b = take_b.astype(jnp.bfloat16)
            got_a, got_b = sent_together_2((send_a, send_b), "grp", 0, 0, 1)
            ahead = jnp.sum(got_a.astype(jnp.float32), 0).astype(jnp.bfloat16)
            behind = jnp.sum(got_b.astype(jnp.float32), 0).astype(jnp.bfloat16)
        block = jnp.concatenate([ahead, behind], axis=0)
        user_b = users.astype(jnp.bfloat16)
        pred = lax.dot_general(
            user_b, block, (((1,), (1,)), ((), ())), preferred_element_type=jnp.float32
        )
        err = jnp.where(
            rated[stratum] == 1, pred - ratings[stratum].astype(jnp.float32), 0.0
        ).astype(jnp.bfloat16)
        grad_user = jnp.dot(err, block, preferred_element_type=jnp.float32)
        grad_item = lax.dot_general(
            err, user_b, (((0,), (0,)), ((), ())), preferred_element_type=jnp.float32
        )
        users = users - RATE * (grad_user + DECAY * users)
        block_f = block.astype(jnp.float32)
        block = (block_f - RATE * (grad_item + DECAY * block_f)).astype(jnp.bfloat16)
        ahead = block[:half]
        behind = block[half:]
        if stratum < strata - 1:
            ahead = from_behind(ahead, ("grp", "blk"), 1)
            behind = from_behind(behind, ("grp", "blk"), -1)
    return (users, ahead, behind)


def solution(mesh):
    in_specs = (
        P(None, ("grp", "blk"), None),
        P(None, ("grp", "blk"), None),
        P(("grp", "blk"), None),
        P(("grp", "blk"), None),
        P(("grp", "blk"), None),
        P(),
    )
    out_specs = (P(("grp", "blk"), None), P(("grp", "blk"), None), P(("grp", "blk"), None))
    return jax.shard_map(body, mesh=mesh, in_specs=in_specs, out_specs=out_specs, check_vma=False)
```

profile of v0, /device:TPU:1, one launch (start us, length us, event | category | flops | bytes accessed | tf_op | source)
XLA Modules:
  0.0 283.8 jit_solution(12259282397617947830)
XLA Ops:
  7.2 11.5 %fusion.110 = (s32[1,1024,512]{2,1,0:T(8,128)}, s32[1,1024,512]{2,1,0:T(8,128)}, s32[1,1024,512]{2,1,0:T(8,128)}, s32[1,1024,512]{2,1,0:T(8,128)}, s32[1,1024,51...) fusion(s32[8,1024,512]{2,1,0:T(8,128)} %param.7), kind=kLoop, calls=%fused_computation.148 | loop fusion | bytes 33554432 | tf_op jit(solution)/shard_map/slice | solution.py:74
  18.7 1.9 copy.67
  20.6 6.0 %fusion.111 = (bf16[1,1024,512]{2,1,0:T(8,128)(2,1)}, bf16[1,1024,512]{2,1,0:T(8,128)(2,1)}, bf16[1,1024,512]{2,1,0:T(8,128)(2,1)}, bf16[1,1024,512]{2,1,0:T(8,1...) fusion(bf16[8,1024,512]{2,1,0:T(8,128)(2,1)} %param.6), kind=kLoop, calls=%fused_computation.149 | loop fusion | bytes 16777216 | tf_op jit(solution)/shard_map/slice | solution.py:74
  26.6 0.5 copy.68
  27.9 2.1 fusion.19
  30.0 0.5 fusion.46
  30.4 0.7 fusion.120
  31.2 3.7 %collective-permute-start = (bf16[256,256]{1,0:T(8,128)(2,1)}, bf16[256,256]{1,0:T(8,128)(2,1)}, u32[]{:S(2)}, u32[]{:S(2)}) collective-permute-start(bf16[256,256]{1,0:T(8,128)(2,1)} %get-tuple-element.38), channel_id=1, source_target_pairs={{0,1},{1,2},{2,3},{3,4},{4,5},{5,6},{6,7},{7,8},{8,9},{9,10},{10,1... | collective-permute-start | bytes 393224 | tf_op jit(solution)/shard_map/ppermute | solution.py:36
  34.9 6.2 %collective-permute-start.1 = (bf16[256,256]{1,0:T(8,128)(2,1)}, bf16[256,256]{1,0:T(8,128)(2,1)S(1)}, u32[]{:S(2)}, u32[]{:S(2)}) collective-permute-start(bf16[256,256]{1,0:T(8,128)(2,1)} %get-tuple-element.37), channel_id=1, source_target_pairs={{0,127},{1,0},{2,1},{3,2},{4,3},{5,4},{6,5},{7,6},{8,7},{9,8},{10,... | collective-permute-start | bytes 393224 | tf_op jit(solution)/shard_map/ppermute | solution.py:36
  41.1 0.5 fusion.35
  41.6 3.0 %copy.69 = s32[1,1024,512]{1,2,0:T(8,128)} copy(s32[1,1024,512]{2,1,0:T(8,128)} %get-tuple-element.11) | data formatting | bytes 4194304
  44.6 2.4 copy.70
  47.0 1.8 copy.71
  48.9 2.4 copy.72
  51.3 1.8 copy.73
  53.1 2.4 copy.74
  55.6 0.9 constant_dynamic-update-slice_fusion.3
  56.5 1.8 fusion.17
  58.3 0.5 fusion.50
  58.9 7.5 %collective-permute-start.3 = (bf16[256,256]{1,0:T(8,128)(2,1)S(1)}, bf16[256,256]{1,0:T(8,128)(2,1)S(1)}, u32[]{:S(2)}, u32[]{:S(2)}) collective-permute-start(bf16[256,256]{1,0:T(8,128)(2,1)S(1)} %get-tuple-element.35), channel_id=1, source_target_pairs={{0,127},{1,0},{2,1},{3,2},{4,3},{5,4},{6,5},{7,6},{8,7},{9,8},{10,... | collective-permute-start | bytes 393224 | tf_op jit(solution)/shard_map/ppermute | solution.py:36
  66.4 0.5 fusion.33
  66.8 2.4 collective-permute-done.2
  69.3 0.5 fusion.15
  70.4 8.3 %collective-permute-start.5 = (bf16[256,256]{1,0:T(8,128)(2,1)S(1)}, bf16[256,256]{1,0:T(8,128)(2,1)S(1)}, u32[]{:S(2)}, u32[]{:S(2)}) collective-permute-start(bf16[256,256]{1,0:T(8,128)(2,1)S(1)} %get-tuple-element.33), channel_id=1, source_target_pairs={{0,127},{1,0},{2,1},{3,2},{4,3},{5,4},{6,5},{7,6},{8,7},{9,8},{10,... | collective-permute-start | bytes 393224 | tf_op jit(solution)/shard_map/ppermute | solution.py:36
  78.6 0.5 fusion.31
  79.1 2.6 collective-permute-done.4
  81.7 0.5 fusion.13
  82.7 8.4 %collective-permute-start.7 = (bf16[256,256]{1,0:T(8,128)(2,1)S(1)}, bf16[256,256]{1,0:T(8,128)(2,1)S(1)}, u32[]{:S(2)}, u32[]{:S(2)}) collective-permute-start(bf16[256,256]{1,0:T(8,128)(2,1)S(1)} %get-tuple-element.32), channel_id=1, source_target_pairs={{0,127},{1,0},{2,1},{3,2},{4,3},{5,4},{6,5},{7,6},{8,7},{9,8},{10,... | collective-permute-start | bytes 393224 | tf_op jit(solution)/shard_map/ppermute | solution.py:36
  91.1 3.2 %collective-permute-done.7 = bf16[256,256]{1,0:T(8,128)(2,1)S(1)} collective-permute-done((bf16[256,256]{1,0:T(8,128)(2,1)S(1)}, bf16[256,256]{1,0:T(8,128)(2,1)S(1)}, u32[]{:S(2)}, u32[]{:S(2)}) %collective-permute-start.7) | collective-permute-done | bytes 131104 | tf_op jit(solution)/shard_map/ppermute | solution.py:36
  94.3 7.7 %collective-permute-done.6 = bf16[256,256]{1,0:T(8,128)(2,1)S(1)} collective-permute-done((bf16[256,256]{1,0:T(8,128)(2,1)S(1)}, bf16[256,256]{1,0:T(8,128)(2,1)S(1)}, u32[]{:S(2)}, u32[]{:S(2)}) %collective-permute-start.6) | collective-permute-done | bytes 131104 | tf_op jit(solution)/shard_map/ppermute | solution.py:36
  102.0 0.7 pad_maximum_fusion.1
  102.8 96.6 %all-gather.2.cloned.1.call-done = bf16[8192,512]{1,0:T(8,128)(2,1)} async-done(((bf16[256,512]{1,0:T(8,128)(2,1)}), bf16[8192,512]{1,0:T(8,128)(2,1)}) %all-gather.2.cloned.1.call-update) | async-done | bytes 8388624 | tf_op jit(solution)/shard_map/all_gather | solution.py:16
  199.4 3.8 %fusion.112 = (bf16[8192,256]{1,0:T(8,128)(2,1)S(1)}, bf16[8192,256]{1,0:T(8,128)(2,1)S(1)}) fusion(bf16[8192,512]{1,0:T(8,128)(2,1)} %all-gather.2.cloned.1.call-done), kind=kLoop, calls=%fused_computation.150 | loop fusion | bytes 16777216 | tf_op jit(solution)/shard_map/split | solution.py:16
  203.2 2.4 fusion.39
  205.6 2.4 fusion.36
  208.0 0.7 pad_maximum_fusion
  208.7 1.1 copy.48
  209.9 5.6 %all-to-all-start = ((bf16[4,512,256]{2,1,0:T(8,128)(2,1)}), bf16[4,512,256]{2,1,0:T(8,128)(2,1)}, u32[]{:S(2)}, u32[]{:S(2)}) async-start(bf16[4,512,256]{2,1,0:T(8,128)(2,1)} %copy.48), calls=%async_computation | async-start | bytes 2097152 | tf_op jit(solution)/shard_map/all_to_all | solution.py:27
  215.5 3.0 %copy.75 = s32[1,1024,512]{1,2,0:T(8,128)} copy(s32[1,1024,512]{2,1,0:T(8,128)} %get-tuple-element.8) | data formatting | bytes 4194304
  218.5 1.3 copy.76
  219.8 3.0 %copy.77 = s32[1,1024,512]{1,2,0:T(8,128)} copy(s32[1,1024,512]{2,1,0:T(8,128)} %get-tuple-element.7) | data formatting | bytes 4194304
  222.8 1.3 copy.78
  224.1 3.0 %copy.79 = s32[1,1024,512]{1,2,0:T(8,128)} copy(s32[1,1024,512]{2,1,0:T(8,128)} %get-tuple-element.6) | data formatting | bytes 4194304
  227.1 1.3 copy.80
  228.5 3.0 %copy.81 = s32[1,1024,512]{1,2,0:T(8,128)} copy(s32[1,1024,512]{2,1,0:T(8,128)} %get-tuple-element.5) | data formatting | bytes 4194304
  231.5 1.3 copy.82
  232.8 0.5 fusion.29
  233.3 1.4 slice_reduce_fusion.1
  234.8 2.4 fusion.11
  237.1 0.5 fusion.47
  237.9 7.2 %collective-permute-start.9 = (bf16[256,256]{1,0:T(8,128)(2,1)S(1)}, bf16[256,256]{1,0:T(8,128)(2,1)S(1)}, u32[]{:S(2)}, u32[]{:S(2)}) collective-permute-start(bf16[256,256]{1,0:T(8,128)(2,1)S(1)} %get-tuple-element.29), channel_id=1, source_target_pairs={{0,127},{1,0},{2,1},{3,2},{4,3},{5,4},{6,5},{7,6},{8,7},{9,8},{10,... | collective-permute-start | bytes 393224 | tf_op jit(solution)/shard_map/ppermute | solution.py:36
  245.2 0.5 fusion.27
  245.7 3.7 %collective-permute-done.8 = bf16[256,256]{1,0:T(8,128)(2,1)S(1)} collective-permute-done((bf16[256,256]{1,0:T(8,128)(2,1)S(1)}, bf16[256,256]{1,0:T(8,128)(2,1)S(1)}, u32[]{:S(2)}, u32[]{:S(2)}) %collective-permute-start.8) | collective-permute-done | bytes 131104 | tf_op jit(solution)/shard_map/ppermute | solution.py:36
  249.4 0.5 fusion.9
  250.5 7.5 %collective-permute-start.11 = (bf16[256,256]{1,0:T(8,128)(2,1)S(1)}, bf16[256,256]{1,0:T(8,128)(2,1)S(1)}, u32[]{:S(2)}, u32[]{:S(2)}) collective-permute-start(bf16[256,256]{1,0:T(8,128)(2,1)S(1)} %get-tuple-element.27), channel_id=1, source_target_pairs={{0,127},{1,0},{2,1},{3,2},{4,3},{5,4},{6,5},{7,6},{8,7},{9,8},{10,... | collective-permute-start | bytes 393224 | tf_op jit(solution)/shard_map/ppermute | solution.py:36
  258.0 0.5 fusion.25
  258.5 2.6 collective-permute-done.10
  261.3 0.5 fusion.7
  262.4 8.2 %collective-permute-start.13 = (bf16[256,256]{1,0:T(8,128)(2,1)S(1)}, bf16[256,256]{1,0:T(8,128)(2,1)S(1)}, u32[]{:S(2)}, u32[]{:S(2)}) collective-permute-start(bf16[256,256]{1,0:T(8,128)(2,1)S(1)} %get-tuple-element.25), channel_id=1, source_target_pairs={{0,127},{1,0},{2,1},{3,2},{4,3},{5,4},{6,5},{7,6},{8,7},{9,8},{10,... | collective-permute-start | bytes 393224 | tf_op jit(solution)/shard_map/ppermute | solution.py:36
  270.6 0.5 fusion.23
  271.1 2.7 collective-permute-done.12
  273.9 0.5 fusion.5
  274.4 1.4 fusion.21
  276.3 0.7 fusion.113
  (85 shorter events, 4.2 us)
Async XLA Ops:
  7.2 192.2 %all-gather.2.cloned.1.call-start = ((), (), s32[]{:S(2)}) async-start(), calls=%async_computation.1 | async-start | bytes 8650752 | tf_op jit(solution)/shard_map/all_gather | solution.py:16
  18.7 1.9 copy-start.18
  26.6 0.9 copy-start.19
  26.6 1.3 copy-start
  31.2 24.4 %collective-permute-start = (bf16[256,256]{1,0:T(8,128)(2,1)}, bf16[256,256]{1,0:T(8,128)(2,1)}, u32[]{:S(2)}, u32[]{:S(2)}) collective-permute-start(bf16[256,256]{1,0:T(8,128)(2,1)} %get-tuple-element.38), channel_id=1, source_target_pairs={{0,1},{1,2},{2,3},{3,4},{4,5},{5,6},{6,7},{7,8},{8,9},{9,10},{10,1... | collective-permute-start | bytes 393224 | tf_op jit(solution)/shard_map/ppermute | solution.py:36
  34.9 21.6 %collective-permute-start.1 = (bf16[256,256]{1,0:T(8,128)(2,1)}, bf16[256,256]{1,0:T(8,128)(2,1)S(1)}, u32[]{:S(2)}, u32[]{:S(2)}) collective-permute-start(bf16[256,256]{1,0:T(8,128)(2,1)} %get-tuple-element.37), channel_id=1, source_target_pairs={{0,127},{1,0},{2,1},{3,2},{4,3},{5,4},{6,5},{7,6},{8,7},{9,8},{10,... | collective-permute-start | bytes 393224 | tf_op jit(solution)/shard_map/ppermute | solution.py:36
  44.6 2.5 copy-start.2
  48.9 2.4 copy-start.1
  53.1 3.4 %copy-start.8 = (s32[1,1024,512]{1,2,0:T(8,128)S(1)}, s32[1,1024,512]{1,2,0:T(8,128)}, u32[]{:S(2)}) copy-start(s32[1,1024,512]{1,2,0:T(8,128)} %copy.69) | copy-start | bytes 6291460
  58.8 10.5 %copy-start.7 = (s32[1,1024,512]{1,2,0:T(8,128)S(1)}, s32[1,1024,512]{1,2,0:T(8,128)}, u32[]{:S(2)}) copy-start(s32[1,1024,512]{1,2,0:T(8,128)} %copy.71) | copy-start | bytes 6291460
  58.8 10.5 %copy-start.17 = (bf16[1,1024,512]{1,2,0:T(8,128)(2,1)S(1)}, bf16[1,1024,512]{1,2,0:T(8,128)(2,1)}, u32[]{:S(2)}) copy-start(bf16[1,1024,512]{1,2,0:T(8,128)(2,1)} %copy.72) | copy-start | bytes 3145732
  58.8 10.4 %collective-permute-start.2 = (bf16[256,256]{1,0:T(8,128)(2,1)S(1)}, bf16[256,256]{1,0:T(8,128)(2,1)S(1)}, u32[]{:S(2)}, u32[]{:S(2)}) collective-permute-start(bf16[256,256]{1,0:T(8,128)(2,1)S(1)} %get-tuple-element.36), channel_id=1, source_target_pairs={{0,1},{1,2},{2,3},{3,4},{4,5},{5,6},{6,7},{7,8},{8,9},{9,10},{10,1... | collective-permute-start | bytes 393224 | tf_op jit(solution)/shard_map/ppermute | solution.py:36
  58.9 10.3 %collective-permute-start.3 = (bf16[256,256]{1,0:T(8,128)(2,1)S(1)}, bf16[256,256]{1,0:T(8,128)(2,1)S(1)}, u32[]{:S(2)}, u32[]{:S(2)}) collective-permute-start(bf16[256,256]{1,0:T(8,128)(2,1)S(1)} %get-tuple-element.35), channel_id=1, source_target_pairs={{0,127},{1,0},{2,1},{3,2},{4,3},{5,4},{6,5},{7,6},{8,7},{9,8},{10,... | collective-permute-start | bytes 393224 | tf_op jit(solution)/shard_map/ppermute | solution.py:36
  70.2 11.5 %copy-start.5 = (s32[1,1024,512]{1,2,0:T(8,128)S(1)}, s32[1,1024,512]{1,2,0:T(8,128)}, u32[]{:S(2)}) copy-start(s32[1,1024,512]{1,2,0:T(8,128)} %copy.73) | copy-start | bytes 6291460
  70.3 11.5 %copy-start.15 = (bf16[1,1024,512]{1,2,0:T(8,128)(2,1)S(1)}, bf16[1,1024,512]{1,2,0:T(8,128)(2,1)}, u32[]{:S(2)}) copy-start(bf16[1,1024,512]{1,2,0:T(8,128)(2,1)} %copy.74) | copy-start | bytes 3145732
  70.3 11.4 %collective-permute-start.4 = (bf16[256,256]{1,0:T(8,128)(2,1)S(1)}, bf16[256,256]{1,0:T(8,128)(2,1)S(1)}, u32[]{:S(2)}, u32[]{:S(2)}) collective-permute-start(bf16[256,256]{1,0:T(8,128)(2,1)S(1)} %get-tuple-element.34), channel_id=1, source_target_pairs={{0,1},{1,2},{2,3},{3,4},{4,5},{5,6},{6,7},{7,8},{8,9},{9,10},{10,1... | collective-permute-start | bytes 393224 | tf_op jit(solution)/shard_map/ppermute | solution.py:36
  70.4 11.3 %collective-permute-start.5 = (bf16[256,256]{1,0:T(8,128)(2,1)S(1)}, bf16[256,256]{1,0:T(8,128)(2,1)S(1)}, u32[]{:S(2)}, u32[]{:S(2)}) collective-permute-start(bf16[256,256]{1,0:T(8,128)(2,1)S(1)} %get-tuple-element.33), channel_id=1, source_target_pairs={{0,127},{1,0},{2,1},{3,2},{4,3},{5,4},{6,5},{7,6},{8,7},{9,8},{10,... | collective-permute-start | bytes 393224 | tf_op jit(solution)/shard_map/ppermute | solution.py:36
  82.2 20.5 %copy-start.20 = (s32[2,128]{1,0:T(2,128)S(1)}, s32[2,128]{1,0:T(2,128)}, u32[]{:S(2)}) copy-start(s32[2,128]{1,0:T(2,128)} %param.11) | copy-start | bytes 3076
  82.7 11.5 %collective-permute-start.7 = (bf16[256,256]{1,0:T(8,128)(2,1)S(1)}, bf16[256,256]{1,0:T(8,128)(2,1)S(1)}, u32[]{:S(2)}, u32[]{:S(2)}) collective-permute-start(bf16[256,256]{1,0:T(8,128)(2,1)S(1)} %get-tuple-element.32), channel_id=1, source_target_pairs={{0,127},{1,0},{2,1},{3,2},{4,3},{5,4},{6,5},{7,6},{8,7},{9,8},{10,... | collective-permute-start | bytes 393224 | tf_op jit(solution)/shard_map/ppermute | solution.py:36
  91.1 10.9 %collective-permute-start.6 = (bf16[256,256]{1,0:T(8,128)(2,1)S(1)}, bf16[256,256]{1,0:T(8,128)(2,1)S(1)}, u32[]{:S(2)}, u32[]{:S(2)}) collective-permute-start(bf16[256,256]{1,0:T(8,128)(2,1)S(1)} %get-tuple-element.31), channel_id=1, source_target_pairs={{0,1},{1,2},{2,3},{3,4},{4,5},{5,6},{6,7},{7,8},{8,9},{9,10},{10,1... | collective-permute-start | bytes 393224 | tf_op jit(solution)/shard_map/ppermute | solution.py:36
  209.9 23.4 %all-to-all-start = ((bf16[4,512,256]{2,1,0:T(8,128)(2,1)}), bf16[4,512,256]{2,1,0:T(8,128)(2,1)}, u32[]{:S(2)}, u32[]{:S(2)}) async-start(bf16[4,512,256]{2,1,0:T(8,128)(2,1)} %copy.48), calls=%async_computation | async-start | bytes 2097152 | tf_op jit(solution)/shard_map/all_to_all | solution.py:27
  215.5 3.0 %copy-start.12 = (bf16[1,1024,512]{2,1,0:T(8,128)(2,1)S(1)}, bf16[1,1024,512]{2,1,0:T(8,128)(2,1)}, u32[]{:S(2)}) copy-start(bf16[1,1024,512]{2,1,0:T(8,128)(2,1)} %get-tuple-element.16) | copy-start | bytes 3145732
  219.8 3.0 %copy-start.11 = (bf16[1,1024,512]{2,1,0:T(8,128)(2,1)S(1)}, bf16[1,1024,512]{2,1,0:T(8,128)(2,1)}, u32[]{:S(2)}) copy-start(bf16[1,1024,512]{2,1,0:T(8,128)(2,1)} %get-tuple-element.15) | copy-start | bytes 3145732
  224.1 3.0 %copy-start.10 = (bf16[1,1024,512]{2,1,0:T(8,128)(2,1)S(1)}, bf16[1,1024,512]{2,1,0:T(8,128)(2,1)}, u32[]{:S(2)}) copy-start(bf16[1,1024,512]{2,1,0:T(8,128)(2,1)} %get-tuple-element.14) | copy-start | bytes 3145732
  228.5 3.1 %copy-start.9 = (bf16[1,1024,512]{2,1,0:T(8,128)(2,1)S(1)}, bf16[1,1024,512]{2,1,0:T(8,128)(2,1)}, u32[]{:S(2)}) copy-start(bf16[1,1024,512]{2,1,0:T(8,128)(2,1)} %get-tuple-element.13) | copy-start | bytes 3145732
  237.6 11.8 %copy-start.6 = (s32[1,1024,512]{1,2,0:T(8,128)S(1)}, s32[1,1024,512]{1,2,0:T(8,128)}, u32[]{:S(2)}) copy-start(s32[1,1024,512]{1,2,0:T(8,128)} %copy.77) | copy-start | bytes 6291460
  237.6 11.8 %copy-start.16 = (bf16[1,1024,512]{1,2,0:T(8,128)(2,1)S(1)}, bf16[1,1024,512]{1,2,0:T(8,128)(2,1)}, u32[]{:S(2)}) copy-start(bf16[1,1024,512]{1,2,0:T(8,128)(2,1)} %copy.78) | copy-start | bytes 3145732
  237.6 11.7 %collective-permute-start.8 = (bf16[256,256]{1,0:T(8,128)(2,1)S(1)}, bf16[256,256]{1,0:T(8,128)(2,1)S(1)}, u32[]{:S(2)}, u32[]{:S(2)}) collective-permute-start(bf16[256,256]{1,0:T(8,128)(2,1)S(1)} %get-tuple-element.30), channel_id=1, source_target_pairs={{0,1},{1,2},{2,3},{3,4},{4,5},{5,6},{6,7},{7,8},{8,9},{9,10},{10,1... | collective-permute-start | bytes 393224 | tf_op jit(solution)/shard_map/ppermute | solution.py:36
  237.9 11.5 %collective-permute-start.9 = (bf16[256,256]{1,0:T(8,128)(2,1)S(1)}, bf16[256,256]{1,0:T(8,128)(2,1)S(1)}, u32[]{:S(2)}, u32[]{:S(2)}) collective-permute-start(bf16[256,256]{1,0:T(8,128)(2,1)S(1)} %get-tuple-element.29), channel_id=1, source_target_pairs={{0,127},{1,0},{2,1},{3,2},{4,3},{5,4},{6,5},{7,6},{8,7},{9,8},{10,... | collective-permute-start | bytes 393224 | tf_op jit(solution)/shard_map/ppermute | solution.py:36
  250.4 10.8 %copy-start.4 = (s32[1,1024,512]{1,2,0:T(8,128)S(1)}, s32[1,1024,512]{1,2,0:T(8,128)}, u32[]{:S(2)}) copy-start(s32[1,1024,512]{1,2,0:T(8,128)} %copy.79) | copy-start | bytes 6291460
  250.4 10.8 %copy-start.14 = (bf16[1,1024,512]{1,2,0:T(8,128)(2,1)S(1)}, bf16[1,1024,512]{1,2,0:T(8,128)(2,1)}, u32[]{:S(2)}) copy-start(bf16[1,1024,512]{1,2,0:T(8,128)(2,1)} %copy.80) | copy-start | bytes 3145732
  250.4 10.7 %collective-permute-start.10 = (bf16[256,256]{1,0:T(8,128)(2,1)S(1)}, bf16[256,256]{1,0:T(8,128)(2,1)S(1)}, u32[]{:S(2)}, u32[]{:S(2)}) collective-permute-start(bf16[256,256]{1,0:T(8,128)(2,1)S(1)} %get-tuple-element.28), channel_id=1, source_target_pairs={{0,1},{1,2},{2,3},{3,4},{4,5},{5,6},{6,7},{7,8},{8,9},{9,10},{10,1... | collective-permute-start | bytes 393224 | tf_op jit(solution)/shard_map/ppermute | solution.py:36
  250.5 10.7 %collective-permute-start.11 = (bf16[256,256]{1,0:T(8,128)(2,1)S(1)}, bf16[256,256]{1,0:T(8,128)(2,1)S(1)}, u32[]{:S(2)}, u32[]{:S(2)}) collective-permute-start(bf16[256,256]{1,0:T(8,128)(2,1)S(1)} %get-tuple-element.27), channel_id=1, source_target_pairs={{0,127},{1,0},{2,1},{3,2},{4,3},{5,4},{6,5},{7,6},{8,7},{9,8},{10,... | collective-permute-start | bytes 393224 | tf_op jit(solution)/shard_map/ppermute | solution.py:36
  262.2 11.6 %copy-start.3 = (s32[1,1024,512]{1,2,0:T(8,128)S(1)}, s32[1,1024,512]{1,2,0:T(8,128)}, u32[]{:S(2)}) copy-start(s32[1,1024,512]{1,2,0:T(8,128)} %copy.81) | copy-start | bytes 6291460
  262.3 11.6 %copy-start.13 = (bf16[1,1024,512]{1,2,0:T(8,128)(2,1)S(1)}, bf16[1,1024,512]{1,2,0:T(8,128)(2,1)}, u32[]{:S(2)}) copy-start(bf16[1,1024,512]{1,2,0:T(8,128)(2,1)} %copy.82) | copy-start | bytes 3145732
  262.3 11.5 %collective-permute-start.12 = (bf16[256,256]{1,0:T(8,128)(2,1)S(1)}, bf16[256,256]{1,0:T(8,128)(2,1)S(1)}, u32[]{:S(2)}, u32[]{:S(2)}) collective-permute-start(bf16[256,256]{1,0:T(8,128)(2,1)S(1)} %get-tuple-element.26), channel_id=1, source_target_pairs={{0,1},{1,2},{2,3},{3,4},{4,5},{5,6},{6,7},{7,8},{8,9},{9,10},{10,1... | collective-permute-start | bytes 393224 | tf_op jit(solution)/shard_map/ppermute | solution.py:36
  262.4 11.4 %collective-permute-start.13 = (bf16[256,256]{1,0:T(8,128)(2,1)S(1)}, bf16[256,256]{1,0:T(8,128)(2,1)S(1)}, u32[]{:S(2)}, u32[]{:S(2)}) collective-permute-start(bf16[256,256]{1,0:T(8,128)(2,1)S(1)} %get-tuple-element.25), channel_id=1, source_target_pairs={{0,127},{1,0},{2,1},{3,2},{4,3},{5,4},{6,5},{7,6},{8,7},{9,8},{10,... | collective-permute-start | bytes 393224 | tf_op jit(solution)/shard_map/ppermute | solution.py:36
Sparse Core Ops, SparseCore 0:
  102.8 96.5 all-gather.1
where the time goes:
time: 284 us
  waiting for transfers between devices  122 us (43%)
  starting transfers between devices  63.2 us (22%)
  local copies, waits for them, and re-layouts  59.5 us (21%)
  matrix products  21.9 us (8%)
  between operations  14.7 us (5%)
  other arithmetic  2.85 us (1%)
    all_gather x1, waiting for transfers between devices, sent_together(): lax.all_gather(both, axis, axis=dim, tiled=True)  96.6 us
    ppermute x14, starting transfers between devices, from_behind(): lax.ppermute(array, axis, [(i, (i + by) % count) for i in range(count)])  57.6 us
    unnamed x65, local copies, waits for them, and re-layouts  35.5 us
    ppermute x14, waiting for transfers between devices, from_behind(): lax.ppermute(array, axis, [(i, (i + by) % count) for i in range(count)])  25 us
    slice x1, local copies, waits for them, and re-layouts, body(): rated[stratum] == 1  11.5 us
    dot_general x8, matrix products, body(): lax.dot_general(user_b, block, (((1,), (1,)), ((), ())), preferred_elemen...  8.71 us
    slice x1, local copies, waits for them, and re-layouts, body(): ratings[stratum].astype(jnp.float32)  5.96 us
  transfers between devices with their start and end apart: 16, of which 9 were waited for; matrix products, arithmetic and copies ran while one was open for 13% of the time, Pallas kernels for 0%

commit v1 on v0

v1 whole, which is shorter than its diff:
```python
import jax
import jax.numpy as jnp
from jax import lax
from jax.experimental import pallas as pl
from jax.experimental.pallas import tpu as pltpu
from jax.sharding import PartitionSpec as P

RATE = 0.005
DECAY = 0.05
UNRATED = 64.0
AXES = ("grp", "blk")


def code_kernel(rated_ref, ratings_ref, out_ref):
    held = jnp.where(rated_ref[0] == 1, ratings_ref[0].astype(jnp.float32), UNRATED)
    out_ref[...] = held.T.astype(jnp.bfloat16)


def coded(rated, ratings, stratum, tile=256):
    _, users, items = rated.shape
    return pl.pallas_call(
        code_kernel,
        grid=(users // tile,),
        in_specs=[
            pl.BlockSpec((1, tile, items), lambda i: (stratum, i, 0)),
            pl.BlockSpec((1, tile, items), lambda i: (stratum, i, 0)),
        ],
        out_specs=pl.BlockSpec((items, tile), lambda i: (0, i)),
        out_shape=jax.ShapeDtypeStruct((items, users), jnp.bfloat16),
        cost_estimate=pl.CostEstimate(
            flops=users * items, bytes_accessed=users * items * 8, transcendentals=0
        ),
        name=f"code{stratum}",
    )(rated, ratings)


def place_kernel(dest_ref, x_ref, y_ref):
    for j in range(x_ref.shape[0]):
        y_ref[dest_ref[j]] = x_ref[j]


def placed(x, dest):
    return pl.pallas_call(
        place_kernel,
        in_specs=[
            pl.BlockSpec(memory_space=pltpu.SMEM),
            pl.BlockSpec(memory_space=pltpu.VMEM),
        ],
        out_specs=pl.BlockSpec(memory_space=pltpu.VMEM),
        out_shape=jax.ShapeDtypeStruct(x.shape, x.dtype),
        name="place",
    )(dest, x)


def ring(array, by):
    count = lax.axis_size(AXES)
    return lax.ppermute(array, AXES, [(i, (i + by) % count) for i in range(count)])


def all_to_all(x):
    return lax.all_to_all(x, AXES, split_axis=0, concat_axis=0, tiled=True)


def reassigned(ahead, behind, owners):
    half, rank = ahead.shape
    both = jnp.concatenate([ahead, behind], axis=0)
    rows, cols = 2 * half // 8, rank // 128
    tiles = both.reshape(rows, 8, cols, 128).transpose(0, 2, 1, 3).reshape(rows * cols, 8, 128)
    count = rows * cols
    spread = all_to_all(tiles)
    after = jnp.roll(owners[0], -1)
    before = jnp.roll(owners[1], 1)
    dest = jnp.where(lax.axis_index(AXES) < count // 2, after, before)
    got = all_to_all(placed(spread, dest))
    both = got.reshape(rows, cols, 8, 128).transpose(0, 2, 1, 3).reshape(2 * half, rank)
    return both[:half], both[half:]


def errors(code, block, user_b):
    pred = lax.dot_general(
        block, user_b, (((1,), (1,)), ((), ())), preferred_element_type=jnp.float32
    )
    value = code.astype(jnp.float32)
    return jnp.where(value < UNRATED, pred - value, 0.0).astype(jnp.bfloat16)


def updated(block, err, user_b):
    grad = jnp.dot(err, user_b, preferred_element_type=jnp.float32)
    held = block.astype(jnp.float32)
    return (held - RATE * (grad + DECAY * held)).astype(jnp.bfloat16)


def back(err, block):
    return lax.dot_general(
        err, block, (((0,), (0,)), ((), ())), preferred_element_type=jnp.float32
    )


def body(ratings, rated, user_factors, item_ahead, item_behind, owners):
    half = item_ahead.shape[0]
    users, ahead, behind = user_factors, item_ahead, item_behind
    strata = ratings.shape[0]
    for s in range(strata):
        code = coded(rated, ratings, s)
        user_b = users.astype(jnp.bfloat16)
        err_a = errors(code[:half], ahead, user_b)
        new_a = updated(ahead, err_a, user_b)
        err_b = errors(code[half:], behind, user_b)
        new_b = updated(behind, err_b, user_b)
        grad = back(err_a, ahead) + back(err_b, behind)
        users = users - RATE * (grad + DECAY * users)
        ahead, behind = new_a, new_b
        if s == strata // 2 - 1:
            ahead, behind = reassigned(ahead, behind, owners)
        elif s < strata - 1:
            ahead, behind = ring(ahead, 1), ring(behind, -1)
    return users, ahead, behind


def solution(mesh):
    rows = P(AXES, None)
    in_specs = (P(None, AXES, None), P(None, AXES, None), rows, rows, rows, P())
    return jax.shard_map(
        body, mesh=mesh, in_specs=in_specs, out_specs=(rows, rows, rows), check_vma=False
    )
```

time: 284 us -> 172 us (0.61)
  waiting for transfers between devices: 122 us -> 35 us
  local copies, waits for them, and re-layouts: 59.5 us -> 1.43 us
  Pallas kernels: 0 us -> 34 us
  matrix products: 21.9 us -> 36.7 us
  between operations: 14.7 us -> 1.08 us
  starting transfers between devices: 63.2 us -> 58.2 us
    all_gather x1 -> x0, waiting for transfers between devices: 96.6 us -> none  [sent_together(): lax.all_gather(both, axis, axis=dim, tiled=True)]
    unnamed x65 -> x22, local copies, waits for them, and re-layouts: 35.5 us -> 0.75 us
    pallas_call x0 -> x9, Pallas kernels: none -> 34 us  [the longest x8 32.3 us: coded(): pl.pallas_call(code_kernel, grid=(users // tile,), in_specs=[pl.BlockSpec...]
    all_to_all x1 -> x2, waiting for transfers between devices: 0.01 us -> 19.7 us  [all_to_all(): return lax.all_to_all(x, AXES, split_axis=0, concat_axis=0, tiled=True)]
    slice x11 -> x2, local copies, waits for them, and re-layouts: 19 us -> 0.68 us  [reassigned(): before = jnp.roll(owners[1], 1)]
    dot_general x26 -> x48, matrix products: 21.9 us -> 36.7 us  [the longest x16 15.2 us: errors(): lax.dot_general(block, user_b, (((1,), (1,)), ((), ())), preferred_elemen...]
    ppermute x14 -> x12, starting transfers between devices: 57.6 us -> 44.4 us  [ring(): lax.ppermute(array, AXES, [(i, (i + by) % count) for i in range(count)])]
    ppermute x14 -> x12, waiting for transfers between devices: 25 us -> 15.2 us  [ring(): lax.ppermute(array, AXES, [(i, (i + by) % count) for i in range(count)])]
  transfers between devices with their start and end apart: 16 -> 14, of which waited for: 9 -> 9; matrix products, arithmetic and copies ran while one was open for 13% -> 16% of each run, Pallas kernels for 0% -> 17%
where the time goes in v1:
time: 172 us; the launch traced here: 170 us
  starting transfers between devices  58.2 us (34%)
  matrix products  36.7 us (21%)
  waiting for transfers between devices  35 us (20%)
  Pallas kernels  34 us (20%)
  other arithmetic  4.04 us (2%)
    ppermute x12, starting transfers between devices, ring(): lax.ppermute(array, AXES, [(i, (i + by) % count) for i in range(count)])  44.4 us
    pallas_call x8, Pallas kernels, coded(): pl.pallas_call(code_kernel, grid=(users // tile,), in_specs=[pl.BlockSpec...  32.3 us
    all_to_all x2, waiting for transfers between devices, all_to_all(): return lax.all_to_all(x, AXES, split_axis=0, concat_axis=0, tiled=True)  19.7 us
    ppermute x12, waiting for transfers between devices, ring(): lax.ppermute(array, AXES, [(i, (i + by) % count) for i in range(count)])  15.2 us
    dot_general x16, matrix products, errors(): lax.dot_general(block, user_b, (((1,), (1,)), ((), ())), preferred_elemen...  15.2 us
    all_to_all x2, starting transfers between devices, all_to_all(): return lax.all_to_all(x, AXES, split_axis=0, concat_axis=0, tiled=True)  13.8 us
    dot_general x16, matrix products, updated(): grad = jnp.dot(err, user_b, preferred_element_type=jnp.float32)  11.7 us
    dot_general x16, matrix products, back(): lax.dot_general(err, block, (((0,), (0,)), ((), ())), preferred_element_t...  9.77 us
  transfers between devices with their start and end apart: 14, of which 9 were waited for; matrix products, arithmetic and copies ran while one was open for 16% of the time, Pallas kernels for 17%

profile of v1, /device:TPU:1, one launch (start us, length us, event | category | flops | bytes accessed | tf_op | source)
XLA Modules:
  0.0 170.5 jit_solution(7668717062732949962)
XLA Ops:
  0.7 1.3 convert_element_type.217
  2.0 4.0 %code0.1 = bf16[512,1024]{1,0:T(8,128)(2,1)} custom-call(s32[8,1024,512]{2,1,0:T(8,128)} %rated_ref.15, bf16[8,1024,512]{2,1,0:T(8,128)(2,1)} %ratings_ref.15), custom_call_target="tpu_custom_call" | custom-call | flops 524288 | bytes 4194304 | tf_op jit(solution)/shard_map/code0/pallas_call | solution.py:21
  6.1 1.4 fusion.41
  7.4 1.0 fusion.66
  8.4 10.0 %collective-permute-start.1 = (bf16[256,256]{1,0:T(8,128)(2,1)}, bf16[256,256]{1,0:T(8,128)(2,1)S(1)}, u32[]{:S(2)}, u32[]{:S(2)}) collective-permute-start(bf16[256,256]{1,0:T(8,128)(2,1)} %fusion.66), channel_id=1, source_target_pairs={{0,127},{1,0},{2,1},{3,2},{4,3},{5,4},{6,5},{7,6},{8,7},{9,8},{10,... | collective-permute-start | bytes 393224 | tf_op jit(solution)/shard_map/ppermute | solution.py:57
  18.4 1.4 fusion.40
  19.8 1.0 fusion.67
  20.7 0.3 fusion.113
  21.1 1.2 fusion.106
  22.4 0.6 fusion.105
  23.0 4.0 %code1.1 = bf16[512,1024]{1,0:T(8,128)(2,1)} custom-call(s32[8,1024,512]{2,1,0:T(8,128)} %rated_ref.15, bf16[8,1024,512]{2,1,0:T(8,128)(2,1)} %ratings_ref.15), custom_call_target="tpu_custom_call" | custom-call | flops 524288 | bytes 4194304 | tf_op jit(solution)/shard_map/code1/pallas_call | solution.py:21
  27.0 4.0 %code2.1 = bf16[512,1024]{1,0:T(8,128)(2,1)} custom-call(s32[8,1024,512]{2,1,0:T(8,128)} %rated_ref.15, bf16[8,1024,512]{2,1,0:T(8,128)(2,1)} %ratings_ref.15), custom_call_target="tpu_custom_call" | custom-call | flops 524288 | bytes 4194304 | tf_op jit(solution)/shard_map/code2/pallas_call | solution.py:21
  31.0 4.1 %code3.1 = bf16[512,1024]{1,0:T(8,128)(2,1)} custom-call(s32[8,1024,512]{2,1,0:T(8,128)} %rated_ref.15, bf16[8,1024,512]{2,1,0:T(8,128)(2,1)} %ratings_ref.15), custom_call_target="tpu_custom_call" | custom-call | flops 524288 | bytes 4194304 | tf_op jit(solution)/shard_map/code3/pallas_call | solution.py:21
  35.0 4.0 %code4.1 = bf16[512,1024]{1,0:T(8,128)(2,1)} custom-call(s32[8,1024,512]{2,1,0:T(8,128)} %rated_ref.15, bf16[8,1024,512]{2,1,0:T(8,128)(2,1)} %ratings_ref.15), custom_call_target="tpu_custom_call" | custom-call | flops 524288 | bytes 4194304 | tf_op jit(solution)/shard_map/code4/pallas_call | solution.py:21
  39.0 4.0 %code5.1 = bf16[512,1024]{1,0:T(8,128)(2,1)} custom-call(s32[8,1024,512]{2,1,0:T(8,128)} %rated_ref.15, bf16[8,1024,512]{2,1,0:T(8,128)(2,1)} %ratings_ref.15), custom_call_target="tpu_custom_call" | custom-call | flops 524288 | bytes 4194304 | tf_op jit(solution)/shard_map/code5/pallas_call | solution.py:21
  43.0 4.1 %code6.1 = bf16[512,1024]{1,0:T(8,128)(2,1)} custom-call(s32[8,1024,512]{2,1,0:T(8,128)} %rated_ref.15, bf16[8,1024,512]{2,1,0:T(8,128)(2,1)} %ratings_ref.15), custom_call_target="tpu_custom_call" | custom-call | flops 524288 | bytes 4194304 | tf_op jit(solution)/shard_map/code6/pallas_call | solution.py:21
  47.1 4.1 %code7.1 = bf16[512,1024]{1,0:T(8,128)(2,1)} custom-call(s32[8,1024,512]{2,1,0:T(8,128)} %rated_ref.15, bf16[8,1024,512]{2,1,0:T(8,128)(2,1)} %ratings_ref.15), custom_call_target="tpu_custom_call" | custom-call | flops 524288 | bytes 4194304 | tf_op jit(solution)/shard_map/code7/pallas_call | solution.py:21
  51.2 2.0 %broadcast_select_fusion.dest_ref = s32[128]{0:T(128)} fusion(pred[]{:T(512)S(6)} %lt.60, s32[1]{0:T(128)} %bitcast.1, s32[127]{0:T(128)S(1)} %get-tuple-element.6, s32[127]{0:T(128)S(1)} %get-tuple-element.5, s32[1]{0:T(128)} %bitcast.2), kind=kLoop, calls=%fused_computation.180 | loop fusion | flops 384 | bytes 1537 | tf_op jit(solution)/shard_map/jit(_where)/select_n | solution.py:73
  53.3 1.4 fusion.42
  54.6 1.3 fusion.70
  56.1 1.4 fusion.43
  57.5 1.3 fusion.73
  58.8 7.5 %collective-permute-start.3 = (bf16[256,256]{1,0:T(8,128)(2,1)S(1)}, bf16[256,256]{1,0:T(8,128)(2,1)S(1)}, u32[]{:S(2)}, u32[]{:S(2)}) collective-permute-start(bf16[256,256]{1,0:T(8,128)(2,1)S(1)} %fusion.73), channel_id=1, source_target_pairs={{0,127},{1,0},{2,1},{3,2},{4,3},{5,4},{6,5},{7,6},{8,7},{9,8},{10,... | collective-permute-start | bytes 393224 | tf_op jit(solution)/shard_map/ppermute | solution.py:57
  66.4 0.3 fusion.114
  66.7 0.4 fusion.107
  67.2 0.3 fusion.44
  68.0 1.2 collective-permute-done.3
  69.9 8.3 %collective-permute-start.5 = (bf16[256,256]{1,0:T(8,128)(2,1)S(1)}, bf16[256,256]{1,0:T(8,128)(2,1)S(1)}, u32[]{:S(2)}, u32[]{:S(2)}) collective-permute-start(bf16[256,256]{1,0:T(8,128)(2,1)S(1)} %fusion.79), channel_id=1, source_target_pairs={{0,127},{1,0},{2,1},{3,2},{4,3},{5,4},{6,5},{7,6},{8,7},{9,8},{10,... | collective-permute-start | bytes 393224 | tf_op jit(solution)/shard_map/ppermute | solution.py:57
  78.2 0.3 fusion.115
  78.6 0.4 fusion.108
  79.8 1.5 collective-permute-done.5
  81.9 0.7 pad_maximum_fusion
  82.7 9.5 %all-to-all-start = ((bf16[128,8,128]{2,1,0:T(8,128)(2,1)}), bf16[128,8,128]{2,1,0:T(8,128)(2,1)S(1)}, u32[]{:S(2)}, u32[]{:S(2)}) async-start(bf16[128,8,128]{2,1,0:T(8,128)(2,1)} %bitcast.6), calls=%async_computation | async-start | bytes 524288 | tf_op jit(solution)/shard_map/all_to_all | solution.py:61
  92.1 0.4 fusion.116
  92.5 10.8 %all-to-all-done.x_ref = bf16[128,8,128]{2,1,0:T(8,128)(2,1)S(1)} async-done(((bf16[128,8,128]{2,1,0:T(8,128)(2,1)}), bf16[128,8,128]{2,1,0:T(8,128)(2,1)S(1)}, u32[]{:S(2)}, u32[]{:S(2)}) %all-to-all-start) | async-done | bytes 262176 | tf_op jit(solution)/shard_map/all_to_all | solution.py:61
  103.3 0.7 copy-done.6
  104.0 1.8 %place.1 = bf16[128,8,128]{2,1,0:T(8,128)(2,1)} custom-call(s32[128]{0:T(128)} %broadcast_select_fusion.dest_ref, bf16[128,8,128]{2,1,0:T(8,128)(2,1)} %copy-done.6), custom_call_target="tpu_custom_call" | custom-call | tf_op jit(solution)/shard_map/place/pallas_call | solution.py:43
  105.8 4.3 %all-to-all-start.1 = ((bf16[128,8,128]{2,1,0:T(8,128)(2,1)}), bf16[128,8,128]{2,1,0:T(8,128)(2,1)S(1)}, u32[]{:S(2)}, u32[]{:S(2)}) async-start(bf16[128,8,128]{2,1,0:T(8,128)(2,1)} %place.1), calls=%async_computation.1 | async-start | bytes 524288 | tf_op jit(solution)/shard_map/all_to_all | solution.py:61
  110.1 2.3 %fusion.109 = (bf16[1024,256]{1,0:T(8,128)(2,1)}, f32[1024,256]{1,0:T(8,128)S(1)}) fusion(f32[1024,256]{1,0:T(8,128)S(1)} %get-tuple-element.12, f32[1024,256]{1,0:T(8,128)S(1)} %fusion.116, bf16[256,1024]{1,0:T(8,128)(2,1)} %copy-done.7, bf16[256,256]{1,0:T(8,128)(2,1)S(1)} %collective-permute-done.4), kind=kOutput, calls=%fused_computation.187 | convolution fusion | flops 135790592 | bytes 4325376 | tf_op jit(solution)/shard_map/dot_general | solution.py:94
  112.4 8.9 %all-to-all-done.1 = bf16[128,8,128]{2,1,0:T(8,128)(2,1)S(1)} async-done(((bf16[128,8,128]{2,1,0:T(8,128)(2,1)}), bf16[128,8,128]{2,1,0:T(8,128)(2,1)S(1)}, u32[]{:S(2)}, u32[]{:S(2)}) %all-to-all-start.1) | async-done | bytes 262176 | tf_op jit(solution)/shard_map/all_to_all | solution.py:61
  121.3 1.5 fusion.49
  122.9 1.5 fusion.48
  124.4 0.4 fusion.104
  124.8 1.4 fusion.65
  126.2 1.3 fusion.64
  127.6 1.8 %collective-permute-start.7 = (bf16[256,256]{1,0:T(8,128)(2,1)S(1)}, bf16[256,256]{1,0:T(8,128)(2,1)S(1)}, u32[]{:S(2)}, u32[]{:S(2)}) collective-permute-start(bf16[256,256]{1,0:T(8,128)(2,1)S(1)} %fusion.64), channel_id=1, source_target_pairs={{0,127},{1,0},{2,1},{3,2},{4,3},{5,4},{6,5},{7,6},{8,7},{9,8},{10,... | collective-permute-start | bytes 393224 | tf_op jit(solution)/shard_map/ppermute | solution.py:57
  129.4 1.2 collective-permute-start.6
  130.6 0.4 fusion.110
  131.0 3.0 %collective-permute-done.7 = bf16[256,256]{1,0:T(8,128)(2,1)S(1)} collective-permute-done((bf16[256,256]{1,0:T(8,128)(2,1)S(1)}, bf16[256,256]{1,0:T(8,128)(2,1)S(1)}, u32[]{:S(2)}, u32[]{:S(2)}) %collective-permute-start.7) | collective-permute-done | bytes 131104 | tf_op jit(solution)/shard_map/ppermute | solution.py:57
  134.0 1.4 fusion.51
  135.7 7.0 %collective-permute-start.9 = (bf16[256,256]{1,0:T(8,128)(2,1)S(1)}, bf16[256,256]{1,0:T(8,128)(2,1)S(1)}, u32[]{:S(2)}, u32[]{:S(2)}) collective-permute-start(bf16[256,256]{1,0:T(8,128)(2,1)S(1)} %fusion.91), channel_id=1, source_target_pairs={{0,127},{1,0},{2,1},{3,2},{4,3},{5,4},{6,5},{7,6},{8,7},{9,8},{10,... | collective-permute-start | bytes 393224 | tf_op jit(solution)/shard_map/ppermute | solution.py:57
  142.7 1.4 fusion.50
  144.5 0.4 fusion.117
  144.8 0.4 fusion.111
  145.3 1.4 fusion.53
  147.0 8.2 %collective-permute-start.11 = (bf16[256,256]{1,0:T(8,128)(2,1)S(1)}, bf16[256,256]{1,0:T(8,128)(2,1)S(1)}, u32[]{:S(2)}, u32[]{:S(2)}) collective-permute-start(bf16[256,256]{1,0:T(8,128)(2,1)S(1)} %fusion.97), channel_id=1, source_target_pairs={{0,127},{1,0},{2,1},{3,2},{4,3},{5,4},{6,5},{7,6},{8,7},{9,8},{10,... | collective-permute-start | bytes 393224 | tf_op jit(solution)/shard_map/ppermute | solution.py:57
  155.2 0.4 collective-permute-done.8
  156.4 0.4 fusion.118
  156.8 0.4 fusion.112
  157.6 0.4 fusion.119
  157.9 1.0 fusion.103
  158.9 8.9 %collective-permute-done.10 = bf16[256,256]{1,0:T(8,128)(2,1)S(1)} collective-permute-done((bf16[256,256]{1,0:T(8,128)(2,1)S(1)}, bf16[256,256]{1,0:T(8,128)(2,1)S(1)}, u32[]{:S(2)}, u32[]{:S(2)}) %collective-permute-start.10) | collective-permute-done | bytes 131104 | tf_op jit(solution)/shard_map/ppermute | solution.py:57
  168.1 1.0 fusion.100
  169.1 1.4 fusion.3
  (48 shorter events, 5.1 us)
Async XLA Ops:
  0.6 5.4 %copy-start.8 = (bf16[256,256]{1,0:T(8,128)(2,1)S(1)}, bf16[256,256]{1,0:T(8,128)(2,1)}, u32[]{:S(2)}) copy-start(bf16[256,256]{1,0:T(8,128)(2,1)} %param.10) | copy-start | bytes 393220
  0.6 17.7 %copy-start.9 = (bf16[256,256]{1,0:T(8,128)(2,1)S(1)}, bf16[256,256]{1,0:T(8,128)(2,1)}, u32[]{:S(2)}) copy-start(bf16[256,256]{1,0:T(8,128)(2,1)} %param.9) | copy-start | bytes 393220
  2.0 19.1 %copy-start = (f32[1024,256]{1,0:T(8,128)S(1)}, f32[1024,256]{1,0:T(8,128)}, u32[]{:S(2)}) copy-start(f32[1024,256]{1,0:T(8,128)} %param.8) | copy-start | bytes 3145732
  2.0 20.3 %copy-start.10 = (s32[2,128]{1,0:T(2,128)S(1)}, s32[2,128]{1,0:T(2,128)}, u32[]{:S(2)}) copy-start(s32[2,128]{1,0:T(2,128)} %param.11) | copy-start | bytes 3076
  8.4 47.7 %collective-permute-start.1 = (bf16[256,256]{1,0:T(8,128)(2,1)}, bf16[256,256]{1,0:T(8,128)(2,1)S(1)}, u32[]{:S(2)}, u32[]{:S(2)}) collective-permute-start(bf16[256,256]{1,0:T(8,128)(2,1)} %fusion.66), channel_id=1, source_target_pairs={{0,127},{1,0},{2,1},{3,2},{4,3},{5,4},{6,5},{7,6},{8,7},{9,8},{10,... | collective-permute-start | bytes 393224 | tf_op jit(solution)/shard_map/ppermute | solution.py:57
  20.7 32.5 %collective-permute-start = (bf16[256,256]{1,0:T(8,128)(2,1)}, bf16[256,256]{1,0:T(8,128)(2,1)S(1)}, u32[]{:S(2)}, u32[]{:S(2)}) collective-permute-start(bf16[256,256]{1,0:T(8,128)(2,1)} %fusion.67), channel_id=1, source_target_pairs={{0,1},{1,2},{2,3},{3,4},{4,5},{5,6},{6,7},{7,8},{8,9},{9,10},{10,1... | collective-permute-start | bytes 393224 | tf_op jit(solution)/shard_map/ppermute | solution.py:57
  47.1 6.2 %copy-start.5 = (bf16[512,1024]{1,0:T(8,128)(2,1)S(1)}, bf16[512,1024]{1,0:T(8,128)(2,1)}, u32[]{:S(2)}) copy-start(bf16[512,1024]{1,0:T(8,128)(2,1)} %code1.1) | copy-start | bytes 3145732
  47.1 20.1 %copy-start.4 = (bf16[512,1024]{1,0:T(8,128)(2,1)S(1)}, bf16[512,1024]{1,0:T(8,128)(2,1)}, u32[]{:S(2)}) copy-start(bf16[512,1024]{1,0:T(8,128)(2,1)} %code2.1) | copy-start | bytes 3145732
  51.2 27.8 %copy-start.3 = (bf16[512,1024]{1,0:T(8,128)(2,1)S(1)}, bf16[512,1024]{1,0:T(8,128)(2,1)}, u32[]{:S(2)}) copy-start(bf16[512,1024]{1,0:T(8,128)(2,1)} %code3.1) | copy-start | bytes 3145732
  56.0 11.2 %collective-permute-start.2 = (bf16[256,256]{1,0:T(8,128)(2,1)S(1)}, bf16[256,256]{1,0:T(8,128)(2,1)S(1)}, u32[]{:S(2)}, u32[]{:S(2)}) collective-permute-start(bf16[256,256]{1,0:T(8,128)(2,1)S(1)} %fusion.70), channel_id=1, source_target_pairs={{0,1},{1,2},{2,3},{3,4},{4,5},{5,6},{6,7},{7,8},{8,9},{9,10},{10,1... | collective-permute-start | bytes 393224 | tf_op jit(solution)/shard_map/ppermute | solution.py:57
  58.8 10.4 %collective-permute-start.3 = (bf16[256,256]{1,0:T(8,128)(2,1)S(1)}, bf16[256,256]{1,0:T(8,128)(2,1)S(1)}, u32[]{:S(2)}, u32[]{:S(2)}) collective-permute-start(bf16[256,256]{1,0:T(8,128)(2,1)S(1)} %fusion.73), channel_id=1, source_target_pairs={{0,127},{1,0},{2,1},{3,2},{4,3},{5,4},{6,5},{7,6},{8,7},{9,8},{10,... | collective-permute-start | bytes 393224 | tf_op jit(solution)/shard_map/ppermute | solution.py:57
  67.9 11.2 %collective-permute-start.4 = (bf16[256,256]{1,0:T(8,128)(2,1)S(1)}, bf16[256,256]{1,0:T(8,128)(2,1)S(1)}, u32[]{:S(2)}, u32[]{:S(2)}) collective-permute-start(bf16[256,256]{1,0:T(8,128)(2,1)S(1)} %fusion.76), channel_id=1, source_target_pairs={{0,1},{1,2},{2,3},{3,4},{4,5},{5,6},{6,7},{7,8},{8,9},{9,10},{10,1... | collective-permute-start | bytes 393224 | tf_op jit(solution)/shard_map/ppermute | solution.py:57
  69.9 11.4 %collective-permute-start.5 = (bf16[256,256]{1,0:T(8,128)(2,1)S(1)}, bf16[256,256]{1,0:T(8,128)(2,1)S(1)}, u32[]{:S(2)}, u32[]{:S(2)}) collective-permute-start(bf16[256,256]{1,0:T(8,128)(2,1)S(1)} %fusion.79), channel_id=1, source_target_pairs={{0,127},{1,0},{2,1},{3,2},{4,3},{5,4},{6,5},{7,6},{8,7},{9,8},{10,... | collective-permute-start | bytes 393224 | tf_op jit(solution)/shard_map/ppermute | solution.py:57
  79.4 2.2 %copy-start.7 = (bf16[256,1024]{1,0:T(8,128)(2,1)}, bf16[256,1024]{1,0:T(8,128)(2,1)S(1)}, u32[]{:S(2)}) copy-start(bf16[256,1024]{1,0:T(8,128)(2,1)S(1)} %fusion.46) | copy-start | bytes 1572868
  82.7 20.7 %all-to-all-start = ((bf16[128,8,128]{2,1,0:T(8,128)(2,1)}), bf16[128,8,128]{2,1,0:T(8,128)(2,1)S(1)}, u32[]{:S(2)}, u32[]{:S(2)}) async-start(bf16[128,8,128]{2,1,0:T(8,128)(2,1)} %bitcast.6), calls=%async_computation | async-start | bytes 524288 | tf_op jit(solution)/shard_map/all_to_all | solution.py:61
  103.3 0.7 copy-start.6
  105.8 15.5 %all-to-all-start.1 = ((bf16[128,8,128]{2,1,0:T(8,128)(2,1)}), bf16[128,8,128]{2,1,0:T(8,128)(2,1)S(1)}, u32[]{:S(2)}, u32[]{:S(2)}) async-start(bf16[128,8,128]{2,1,0:T(8,128)(2,1)} %place.1), calls=%async_computation.1 | async-start | bytes 524288 | tf_op jit(solution)/shard_map/all_to_all | solution.py:61
  112.4 43.2 %copy-start.2 = (bf16[512,1024]{1,0:T(8,128)(2,1)S(1)}, bf16[512,1024]{1,0:T(8,128)(2,1)}, u32[]{:S(2)}) copy-start(bf16[512,1024]{1,0:T(8,128)(2,1)} %code6.1) | copy-start | bytes 3145732
  124.8 32.4 %copy-start.1 = (bf16[512,1024]{1,0:T(8,128)(2,1)S(1)}, bf16[512,1024]{1,0:T(8,128)(2,1)}, u32[]{:S(2)}) copy-start(bf16[512,1024]{1,0:T(8,128)(2,1)} %code7.1) | copy-start | bytes 3145732
  127.6 6.4 %collective-permute-start.7 = (bf16[256,256]{1,0:T(8,128)(2,1)S(1)}, bf16[256,256]{1,0:T(8,128)(2,1)S(1)}, u32[]{:S(2)}, u32[]{:S(2)}) collective-permute-start(bf16[256,256]{1,0:T(8,128)(2,1)S(1)} %fusion.64), channel_id=1, source_target_pairs={{0,127},{1,0},{2,1},{3,2},{4,3},{5,4},{6,5},{7,6},{8,7},{9,8},{10,... | collective-permute-start | bytes 393224 | tf_op jit(solution)/shard_map/ppermute | solution.py:57
  129.4 13.3 %collective-permute-start.6 = (bf16[256,256]{1,0:T(8,128)(2,1)S(1)}, bf16[256,256]{1,0:T(8,128)(2,1)S(1)}, u32[]{:S(2)}, u32[]{:S(2)}) collective-permute-start(bf16[256,256]{1,0:T(8,128)(2,1)S(1)} %fusion.65), channel_id=1, source_target_pairs={{0,1},{1,2},{2,3},{3,4},{4,5},{5,6},{6,7},{7,8},{8,9},{9,10},{10,1... | collective-permute-start | bytes 393224 | tf_op jit(solution)/shard_map/ppermute | solution.py:57
  135.7 9.6 %collective-permute-start.9 = (bf16[256,256]{1,0:T(8,128)(2,1)S(1)}, bf16[256,256]{1,0:T(8,128)(2,1)S(1)}, u32[]{:S(2)}, u32[]{:S(2)}) collective-permute-start(bf16[256,256]{1,0:T(8,128)(2,1)S(1)} %fusion.91), channel_id=1, source_target_pairs={{0,127},{1,0},{2,1},{3,2},{4,3},{5,4},{6,5},{7,6},{8,7},{9,8},{10,... | collective-permute-start | bytes 393224 | tf_op jit(solution)/shard_map/ppermute | solution.py:57
  144.4 11.3 %collective-permute-start.8 = (bf16[256,256]{1,0:T(8,128)(2,1)S(1)}, bf16[256,256]{1,0:T(8,128)(2,1)S(1)}, u32[]{:S(2)}, u32[]{:S(2)}) collective-permute-start(bf16[256,256]{1,0:T(8,128)(2,1)S(1)} %fusion.88), channel_id=1, source_target_pairs={{0,1},{1,2},{2,3},{3,4},{4,5},{5,6},{6,7},{7,8},{8,9},{9,10},{10,1... | collective-permute-start | bytes 393224 | tf_op jit(solution)/shard_map/ppermute | solution.py:57
  147.0 10.2 %collective-permute-start.11 = (bf16[256,256]{1,0:T(8,128)(2,1)S(1)}, bf16[256,256]{1,0:T(8,128)(2,1)S(1)}, u32[]{:S(2)}, u32[]{:S(2)}) collective-permute-start(bf16[256,256]{1,0:T(8,128)(2,1)S(1)} %fusion.97), channel_id=1, source_target_pairs={{0,127},{1,0},{2,1},{3,2},{4,3},{5,4},{6,5},{7,6},{8,7},{9,8},{10,... | collective-permute-start | bytes 393224 | tf_op jit(solution)/shard_map/ppermute | solution.py:57
  156.3 11.5 %collective-permute-start.10 = (bf16[256,256]{1,0:T(8,128)(2,1)S(1)}, bf16[256,256]{1,0:T(8,128)(2,1)S(1)}, u32[]{:S(2)}, u32[]{:S(2)}) collective-permute-start(bf16[256,256]{1,0:T(8,128)(2,1)S(1)} %fusion.94), channel_id=1, source_target_pairs={{0,1},{1,2},{2,3},{3,4},{4,5},{5,6},{6,7},{7,8},{8,9},{9,10},{10,1... | collective-permute-start | bytes 393224 | tf_op jit(solution)/shard_map/ppermute | solution.py:57

commit v2 on v1

v2 whole, which is shorter than its diff:
```python
import functools

import jax
import jax.numpy as jnp
from jax import lax
from jax.experimental import pallas as pl
from jax.experimental.pallas import tpu as pltpu
from jax.sharding import PartitionSpec as P


RATE = 0.005
DECAY = 0.05
UNRATED = 64.0
AXES = ("grp", "blk")


ANY = pl.BlockSpec(memory_space=pl.ANY)
FAST = pl.BlockSpec(memory_space=pltpu.VMEM)


def marked(rated, ratings):
    return jnp.where(rated == 1, ratings.astype(jnp.float32), UNRATED).astype(jnp.bfloat16)


def own_parity():
    return lax.axis_index("blk") & 1


def code_kernel(start, rated, ratings, token, out, rated_buf, ratings_buf, sems):
    slots, tile, items = rated_buf.shape
    half, parts = items // 2, out.shape[2] // tile

    def fetches(slot, stratum, part):
        rows = pl.ds(pl.multiple_of(part * tile, tile), tile)
        return (
            pltpu.make_async_copy(rated.at[stratum, rows], rated_buf.at[slot], sems.at[0, slot]),
            pltpu.make_async_copy(ratings.at[stratum, rows], ratings_buf.at[slot], sems.at[1, slot]),
        )

    for slot in range(slots):
        for fetch in fetches(slot, start + slot // parts, slot % parts):
            fetch.start()
    parity = own_parity()

    def code(slot, carry):
        t, part = slot // parts, lax.rem(slot, parts)
        for fetch in fetches(slot, start + t, part):
            fetch.wait()
        held = marked(rated_buf[slot], ratings_buf[slot])
        rows = pl.ds(pl.multiple_of(part * tile, tile), tile)
        out[t, parity, rows, :] = held[:, :half]
        out[t, 1 - parity, rows, :] = held[:, half:]
        return carry

    lax.fori_loop(0, slots, code, 0)


def coded(rated, ratings, start, stop, token, tile=256):
    _, users, items = rated.shape
    count = stop - start
    slots = count * (users // tile)
    return pl.pallas_call(
        functools.partial(code_kernel, start),
        in_specs=[ANY, ANY, ANY],
        out_specs=FAST,
        out_shape=jax.ShapeDtypeStruct((count, 2, users, items // 2), jnp.bfloat16),
        scratch_shapes=[
            pltpu.VMEM((slots, tile, items), jnp.int32),
            pltpu.VMEM((slots, tile, items), jnp.bfloat16),
            pltpu.SemaphoreType.DMA((2, slots)),
        ],
        compiler_params=pltpu.CompilerParams(vmem_limit_bytes=(count * 4 + 2) << 20),
        cost_estimate=pl.CostEstimate(
            flops=count * users * items,
            bytes_accessed=count * users * items * 8,
            transcendentals=0,
        ),
    )(rated, ratings, token)


def half_kernel(plane, tile, rated, ratings, token, out, rated_buf, ratings_buf, sems):
    half = out.shape[1]
    cols = pl.ds(pl.multiple_of((own_parity() ^ plane) * half, half), half)
    coming = []
    for i in range(out.shape[0] // tile):
        rows = pl.ds(i * tile, tile)
        pair = (
            pltpu.make_async_copy(rated.at[0, rows, cols], rated_buf.at[rows], sems.at[0, i]),
            pltpu.make_async_copy(ratings.at[0, rows, cols], ratings_buf.at[rows], sems.at[1, i]),
        )
        for fetch in pair:
            fetch.start()
        coming.append((rows, pair))
    for rows, pair in coming:
        for fetch in pair:
            fetch.wait()
        out[rows, :] = marked(rated_buf[rows, :], ratings_buf[rows, :])


def first_kernel(plane, tile, rated, ratings, users_in, ahead, behind, out, users, user_b, blocks,
                 rated_buf, ratings_buf, sems, more_sems):
    parity = own_parity()
    others = (
        pltpu.make_async_copy(users_in, users, more_sems.at[0]),
        pltpu.make_async_copy(ahead, blocks.at[parity], more_sems.at[1]),
        pltpu.make_async_copy(behind, blocks.at[1 - parity], more_sems.at[2]),
    )
    for other in others:
        other.start()
    half_kernel(plane, tile, rated, ratings, None, out, rated_buf, ratings_buf, sems)
    for other in others:
        other.wait()
    user_b[...] = users[...].astype(jnp.bfloat16)


def half_scratch(users, half, tile):
    return [
        pltpu.VMEM((users, half), jnp.int32),
        pltpu.VMEM((users, half), jnp.bfloat16),
        pltpu.SemaphoreType.DMA((2, users // tile)),
    ]


def opened(rated, ratings, users, ahead, behind, plane, tile=256):
    count, rank = users.shape
    half = ahead.shape[0]
    return pl.pallas_call(
        functools.partial(first_kernel, plane, tile),
        in_specs=[ANY] * 5,
        out_specs=[FAST] * 4,
        out_shape=[
            jax.ShapeDtypeStruct((count, half), jnp.bfloat16),
            jax.ShapeDtypeStruct((count, rank), jnp.float32),
            jax.ShapeDtypeStruct((count, rank), jnp.bfloat16),
            jax.ShapeDtypeStruct((2, half, rank), jnp.bfloat16),
        ],
        scratch_shapes=half_scratch(count, half, tile) + [pltpu.SemaphoreType.DMA((3,))],
        compiler_params=pltpu.CompilerParams(vmem_limit_bytes=8 << 20),
        name="opened",
    )(rated, ratings, users, ahead, behind)


def coded_half(rated, ratings, plane, token, tile=256):
    _, users, items = rated.shape
    half = items // 2
    return pl.pallas_call(
        functools.partial(half_kernel, plane, tile),
        in_specs=[ANY] * 3,
        out_specs=FAST,
        out_shape=jax.ShapeDtypeStruct((users, half), jnp.bfloat16),
        scratch_shapes=half_scratch(users, half, tile),
        compiler_params=pltpu.CompilerParams(vmem_limit_bytes=4 << 20),
        cost_estimate=pl.CostEstimate(
            flops=users * half, bytes_accessed=users * half * 8, transcendentals=0
        ),
        name="rest",
    )(rated, ratings, token)


def place_kernel(owners, x, y):
    count = x.shape[0]
    me = lax.axis_index("grp") * lax.axis_size("blk") + lax.axis_index("blk")
    row = jnp.where(me < count // 2, 0, 1)
    step = jnp.where(me < count // 2, 1, count - 1)
    for j in range(count):
        y[owners[row, lax.rem(j + step, count)]] = x[j]


def placed(x, owners):
    return pl.pallas_call(
        place_kernel,
        in_specs=[pl.BlockSpec(memory_space=pltpu.SMEM), FAST],
        out_specs=FAST,
        out_shape=jax.ShapeDtypeStruct(x.shape, x.dtype),
        compiler_params=pltpu.CompilerParams(vmem_limit_bytes=2 << 20),
        name="place",
    )(owners, x)


def over_even(array):
    count = lax.axis_size(AXES)
    return lax.ppermute(array, AXES, [(i, i ^ 1) for i in range(count)])


def over_odd(array):
    count = lax.axis_size(AXES)
    pairs = [(i, (i + 1 if i % 2 else i - 1) % count) for i in range(count)]
    return lax.ppermute(array, AXES, pairs)


MOVES = (over_even, over_odd)
FIRST = (1, 0, 1, 0)
CODED = {0: (1, 4), 3: (4, 5), 4: (5, 8)}


def all_to_all(x):
    return lax.all_to_all(x, AXES, split_axis=0, concat_axis=0, tiled=True)


def reassigned(ahead, behind, owners):
    half, rank = ahead.shape
    both = jnp.concatenate([ahead, behind], axis=0)
    rows, cols = 2 * half // 8, rank // 128
    tiles = both.reshape(rows, 8, cols, 128).transpose(0, 2, 1, 3).reshape(rows * cols, 8, 128)
    spread = all_to_all(tiles)
    sorted_tiles = placed(spread, owners)
    got = all_to_all(sorted_tiles)
    both = got.reshape(rows, cols, 8, 128).transpose(0, 2, 1, 3).reshape(2 * half, rank)
    return both[:half], both[half:]


def errors(code, block, user_b):
    pred = lax.dot_general(
        user_b, block, (((1,), (1,)), ((), ())), preferred_element_type=jnp.float32
    )
    value = code.astype(jnp.float32)
    return jnp.where(value < UNRATED, pred - value, 0.0).astype(jnp.bfloat16)


def updated(block, err, user_b):
    grad = lax.dot_general(
        err, user_b, (((0,), (0,)), ((), ())), preferred_element_type=jnp.float32
    )
    held = block.astype(jnp.float32)
    return (held - RATE * (grad + DECAY * held)).astype(jnp.bfloat16)


def back(err, block):
    return jnp.dot(err, block, preferred_element_type=jnp.float32)


def body(ratings, rated, user_factors, item_ahead, item_behind, owners):
    def held(x):
        return pltpu.with_memory_space_constraint(x, pltpu.HBM)

    rated, ratings = held(rated), held(ratings)
    strata = ratings.shape[0]
    middle = strata // 2
    even, item_ahead = lax.optimization_barrier((own_parity() == 0, item_ahead))

    def swapped(a, b):
        return jnp.where(even, a, b), jnp.where(even, b, a)

    code, users, user_b, blocks = opened(
        rated, ratings, held(user_factors), held(item_ahead), held(item_behind), FIRST[0]
    )
    codes = [None] * strata
    codes[0] = [code, code]
    for s in range(strata):
        first = FIRST[s % 4]
        second = 1 - first
        stays = s in (middle - 1, strata - 1)
        errs, moved, came = [None, None], [None, None], [None, None]
        if s > 0:
            user_b = users.astype(jnp.bfloat16)
        errs[first] = errors(codes[s][first], blocks[first], user_b)
        moved[first] = updated(blocks[first], errs[first], user_b)
        if not stays:
            came[second] = MOVES[first](moved[first])
        moved[first], user_c = lax.optimization_barrier((moved[first], user_b))
        if s == 0:
            codes[0][second] = coded_half(rated, ratings, second, moved[first])
        errs[second] = errors(codes[s][second], blocks[second], user_c)
        moved[second] = updated(blocks[second], errs[second], user_c)
        if not stays:
            came[first] = MOVES[second](moved[second])
        if s in CODED:
            start, stop = CODED[s]
            codes[start:stop] = coded(rated, ratings, start, stop, moved[second])
        grad = back(errs[0], blocks[0]) + back(errs[1], blocks[1])
        users = users - RATE * (grad + DECAY * users)
        if s == middle - 1:
            came = swapped(*reassigned(*swapped(*moved), owners))
        blocks = came
    ahead, behind = swapped(*moved)
    return users, ahead, behind


def solution(mesh):
    rows = P(AXES, None)
    in_specs = (P(None, AXES, None), P(None, AXES, None), rows, rows, rows, P())
    return jax.shard_map(
        body, mesh=mesh, in_specs=in_specs, out_specs=(rows, rows, rows), check_vma=False
    )
```

time: 172 us -> 122 us (0.71)
  starting transfers between devices: 58.2 us -> 36.1 us
  Pallas kernels: 34 us -> 14.9 us
  matrix products: 36.7 us -> 22.7 us
  waiting for transfers between devices: 35 us -> 45.3 us
  other arithmetic: 4.04 us -> 1.55 us
    pallas_call x8 -> x5, Pallas kernels: 32.3 us -> 13.2 us  [the longest x3 9.83 us: coded(): pl.pallas_call(functools.partial(code_kernel, start), in_specs=[ANY, ANY,...]
    ppermute x12, starting transfers between devices: 44.4 us -> 25.9 us  [the longest x6 21.4 us: over_odd(): return lax.ppermute(array, AXES, pairs)]
    dot_general x48, matrix products: 36.7 us -> 22.7 us  [the longest x16 9.56 us: back(): return jnp.dot(err, block, preferred_element_type=jnp.float32)]
    ppermute x12, waiting for transfers between devices: 15.2 us -> 26.8 us  [the longest x6 20.3 us: over_odd(): return lax.ppermute(array, AXES, pairs)]
    all_to_all x2, starting transfers between devices: 13.8 us -> 10.2 us  [all_to_all(): return lax.all_to_all(x, AXES, split_axis=0, concat_axis=0, tiled=True)]
  transfers between devices with their start and end apart: 14 -> 14, of which waited for: 9 -> 9; matrix products, arithmetic and copies ran while one was open for 16% -> 12% of each run, Pallas kernels for 17% -> 8%
where the time goes in v2:
time: 122 us
  waiting for transfers between devices  45.3 us (37%)
  starting transfers between devices  36.1 us (30%)
  matrix products  22.7 us (19%)
  Pallas kernels  14.9 us (12%)
  other arithmetic  1.55 us (1%)
    ppermute x6, starting transfers between devices, over_odd(): return lax.ppermute(array, AXES, pairs)  21.4 us
    ppermute x6, waiting for transfers between devices, over_odd(): return lax.ppermute(array, AXES, pairs)  20.3 us
    all_to_all x2, waiting for transfers between devices, all_to_all(): return lax.all_to_all(x, AXES, split_axis=0, concat_axis=0, tiled=True)  18.4 us
    all_to_all x2, starting transfers between devices, all_to_all(): return lax.all_to_all(x, AXES, split_axis=0, concat_axis=0, tiled=True)  10.2 us
    pallas_call x3, Pallas kernels, coded(): pl.pallas_call(functools.partial(code_kernel, start), in_specs=[ANY, ANY,...  9.83 us
    dot_general x16, matrix products, back(): return jnp.dot(err, block, preferred_element_type=jnp.float32)  9.56 us
    dot_general x16, matrix products, updated(): lax.dot_general(err, user_b, (((0,), (0,)), ((), ())), preferred_element_...  6.65 us
    ppermute x6, waiting for transfers between devices, over_even(): return lax.ppermute(array, AXES, [(i, i ^ 1) for i in range(count)])  6.5 us
  transfers between devices with their start and end apart: 14, of which 9 were waited for; matrix products, arithmetic and copies ran while one was open for 12% of the time, Pallas kernels for 8%

profile of v2, /device:TPU:1, one launch (start us, length us, event | category | flops | bytes accessed | tf_op | source)
XLA Modules:
  0.0 122.1 jit_solution(16087881346512727454)
XLA Ops:
  0.6 1.9 %opened.1 = (bf16[1024,256]{1,0:T(8,128)(2,1)S(1)}, f32[1024,256]{1,0:T(8,128)S(1)}, bf16[1024,256]{1,0:T(8,128)(2,1)S(1)}, bf16[2,256,256]{2,1,0:T(8,128)(2,1)S(1)}) custom-call(s32[8,1024,512]{2,1,0:T(8,128)} %rated.9, bf16[8,1024,512]{2,1,0:T(8,128)(2,1)} %ratings.9, f32[1024,256]{1,0:T(8,128)} %users_in.1, bf16[256,256]{1,0:T(8,128)(2,1)} %ahead, ...), custom_call_target="tpu_custom_call" | custom-call | tf_op jit(solution)/shard_map/opened/pallas_call | solution.py:127
  2.6 0.3 fusion.40
  2.9 0.3 fusion.67.token
  3.3 10.0 %collective-permute-start = (bf16[256,256]{1,0:T(8,128)(2,1)S(1)}, bf16[256,256]{1,0:T(8,128)(2,1)S(1)}, u32[]{:S(2)}, u32[]{:S(2)}) collective-permute-start(bf16[256,256]{1,0:T(8,128)(2,1)S(1)} %fusion.67.token), channel_id=1, source_target_pairs={{0,127},{1,2},{2,1},{3,4},{4,3},{5,6},{6,5},{7,8},{8,7},{9,10},{10... | collective-permute-start | bytes 393224 | tf_op jit(solution)/shard_map/ppermute | solution.py:188
  13.3 1.5 %rest.1 = bf16[1024,256]{1,0:T(8,128)(2,1)S(1)} custom-call(s32[8,1024,512]{2,1,0:T(8,128)} %rated.9, bf16[8,1024,512]{2,1,0:T(8,128)(2,1)} %ratings.9, bf16[256,256]{1,0:T(8,128)(2,1)S(1)} %fusion.67.token), custom_call_target="tpu_custom_call" | custom-call | flops 262144 | bytes 2097152 | tf_op jit(solution)/shard_map/rest/pallas_call | solution.py:146
  14.8 0.3 fusion.41
  15.2 0.4 fusion.66.token
  15.9 0.4 fusion.119
  16.3 3.9 %shard_map.85 = bf16[3,2,1024,256]{3,2,1,0:T(8,128)(2,1)S(1)} custom-call(s32[8,1024,512]{2,1,0:T(8,128)} %rated.9, bf16[8,1024,512]{2,1,0:T(8,128)(2,1)} %ratings.9, bf16[256,256]{1,0:T(8,128)(2,1)S(1)} %fusion.66.token), custom_call_target="tpu_custom_call" | custom-call | flops 1572864 | bytes 12582912 | tf_op jit(solution)/shard_map/pallas_call | solution.py:62
  20.2 0.3 fusion.42
  20.6 0.4 fusion.70
  20.9 3.0 %collective-permute-start.2 = (bf16[256,256]{1,0:T(8,128)(2,1)S(1)}, bf16[256,256]{1,0:T(8,128)(2,1)S(1)}, u32[]{:S(2)}, u32[]{:S(2)}) collective-permute-start(bf16[256,256]{1,0:T(8,128)(2,1)S(1)} %fusion.70), channel_id=1, source_target_pairs={{0,1},{1,0},{2,3},{3,2},{4,5},{5,4},{6,7},{7,6},{8,9},{9,8},{10,11... | collective-permute-start | bytes 393224 | tf_op jit(solution)/shard_map/ppermute | solution.py:182
  23.9 0.3 fusion.43
  24.3 0.4 fusion.76
  24.7 1.7 %collective-permute-start.3 = (bf16[256,256]{1,0:T(8,128)(2,1)S(1)}, bf16[256,256]{1,0:T(8,128)(2,1)S(1)}, u32[]{:S(2)}, u32[]{:S(2)}) collective-permute-start(bf16[256,256]{1,0:T(8,128)(2,1)S(1)} %fusion.76), channel_id=1, source_target_pairs={{0,127},{1,2},{2,1},{3,4},{4,3},{5,6},{6,5},{7,8},{8,7},{9,10},{10... | collective-permute-start | bytes 393224 | tf_op jit(solution)/shard_map/ppermute | solution.py:188
  26.6 0.4 fusion.120
  27.0 2.5 %collective-permute-done.2 = bf16[256,256]{1,0:T(8,128)(2,1)S(1)} collective-permute-done((bf16[256,256]{1,0:T(8,128)(2,1)S(1)}, bf16[256,256]{1,0:T(8,128)(2,1)S(1)}, u32[]{:S(2)}, u32[]{:S(2)}) %collective-permute-start.2) | collective-permute-done | bytes 131104 | tf_op jit(solution)/shard_map/ppermute | solution.py:182
  29.9 0.4 fusion.73
  30.2 4.0 %collective-permute-start.4 = (bf16[256,256]{1,0:T(8,128)(2,1)S(1)}, bf16[256,256]{1,0:T(8,128)(2,1)S(1)}, u32[]{:S(2)}, u32[]{:S(2)}) collective-permute-start(bf16[256,256]{1,0:T(8,128)(2,1)S(1)} %fusion.73), channel_id=1, source_target_pairs={{0,127},{1,2},{2,1},{3,4},{4,3},{5,6},{6,5},{7,8},{8,7},{9,10},{10... | collective-permute-start | bytes 393224 | tf_op jit(solution)/shard_map/ppermute | solution.py:188
  34.2 1.4 %collective-permute-done.3 = bf16[256,256]{1,0:T(8,128)(2,1)S(1)} collective-permute-done((bf16[256,256]{1,0:T(8,128)(2,1)S(1)}, bf16[256,256]{1,0:T(8,128)(2,1)S(1)}, u32[]{:S(2)}, u32[]{:S(2)}) %collective-permute-start.3) | collective-permute-done | bytes 131104 | tf_op jit(solution)/shard_map/ppermute | solution.py:188
  35.6 0.3 fusion.45
  35.9 0.4 fusion.82
  36.7 0.4 fusion.121
  37.1 4.5 %collective-permute-done.4 = bf16[256,256]{1,0:T(8,128)(2,1)S(1)} collective-permute-done((bf16[256,256]{1,0:T(8,128)(2,1)S(1)}, bf16[256,256]{1,0:T(8,128)(2,1)S(1)}, u32[]{:S(2)}, u32[]{:S(2)}) %collective-permute-start.4) | collective-permute-done | bytes 131104 | tf_op jit(solution)/shard_map/ppermute | solution.py:188
  41.6 0.3 fusion.46
  41.9 0.4 fusion.79
  42.3 0.4 copy-done.2
  42.7 0.3 fusion.47
  43.1 0.4 broadcast_select_fusion.3
  43.5 2.0 %shard_map.86 = bf16[1,2,1024,256]{3,2,1,0:T(8,128)(2,1)S(1)} custom-call(s32[8,1024,512]{2,1,0:T(8,128)} %rated.9, bf16[8,1024,512]{2,1,0:T(8,128)(2,1)} %ratings.9, bf16[256,256]{1,0:T(8,128)(2,1)S(1)} %get-tuple-element.38.token), custom_call_target="tpu_custom_call" | custom-call | flops 524288 | bytes 4194304 | tf_op jit(solution)/shard_map/pallas_call | solution.py:62
  45.5 0.7 pad_maximum_fusion
  46.2 5.8 %all-to-all-start = ((bf16[128,8,128]{2,1,0:T(8,128)(2,1)}), bf16[128,8,128]{2,1,0:T(8,128)(2,1)S(1)}, u32[]{:S(2)}, u32[]{:S(2)}) async-start(bf16[128,8,128]{2,1,0:T(8,128)(2,1)} %bitcast.17), calls=%async_computation | async-start | bytes 524288 | tf_op jit(solution)/shard_map/all_to_all | solution.py:197
  52.1 1.4 %fusion.128 = f32[1024,256]{1,0:T(8,128)S(1)} fusion(bf16[1024,256]{1,0:T(8,128)(2,1)} %copy-done.4, bf16[256,256]{1,0:T(8,128)(2,1)} %copy-done.5), kind=kOutput, calls=%fused_computation.220 | convolution fusion | flops 134217728 | bytes 1703936 | tf_op jit(solution)/shard_map/dot_general | solution.py:229
  53.4 9.8 %all-to-all-done.x = bf16[128,8,128]{2,1,0:T(8,128)(2,1)S(1)} async-done(((bf16[128,8,128]{2,1,0:T(8,128)(2,1)}), bf16[128,8,128]{2,1,0:T(8,128)(2,1)S(1)}, u32[]{:S(2)}, u32[]{:S(2)}) %all-to-all-start) | async-done | bytes 262176 | tf_op jit(solution)/shard_map/all_to_all | solution.py:197
  63.2 1.6 %place.1 = bf16[128,8,128]{2,1,0:T(8,128)(2,1)} custom-call(s32[2,128]{1,0:T(2,128)S(1)} %copy-done, bf16[128,8,128]{2,1,0:T(8,128)(2,1)S(1)} %all-to-all-done.x), custom_call_target="tpu_custom_call" | custom-call | tf_op jit(solution)/shard_map/place/pallas_call | solution.py:170
  64.9 4.3 %all-to-all-start.1 = ((bf16[128,8,128]{2,1,0:T(8,128)(2,1)}), bf16[128,8,128]{2,1,0:T(8,128)(2,1)S(1)}, u32[]{:S(2)}, u32[]{:S(2)}) async-start(bf16[128,8,128]{2,1,0:T(8,128)(2,1)} %place.1), calls=%async_computation.1 | async-start | bytes 524288 | tf_op jit(solution)/shard_map/all_to_all | solution.py:197
  69.2 2.6 %fusion.122 = (bf16[1024,256]{1,0:T(8,128)(2,1)}, f32[1024,256]{1,0:T(8,128)}) fusion(f32[1024,256]{1,0:T(8,128)S(1)} %get-tuple-element.48, f32[1024,256]{1,0:T(8,128)S(1)} %fusion.128, bf16[1024,256]{1,0:T(8,128)(2,1)} %copy-done.2, bf16[256,256]{1,0:T(8,128)(2,1)S(1)} %collective-permute-done.4), kind=kOutput, calls=%fused_computation.214 | convolution fusion | flops 135790592 | bytes 4325376 | tf_op jit(solution)/shard_map/dot_general | solution.py:229
  71.8 8.6 %all-to-all-done.1 = bf16[128,8,128]{2,1,0:T(8,128)(2,1)S(1)} async-done(((bf16[128,8,128]{2,1,0:T(8,128)(2,1)}), bf16[128,8,128]{2,1,0:T(8,128)(2,1)S(1)}, u32[]{:S(2)}, u32[]{:S(2)}) %all-to-all-start.1) | async-done | bytes 262176 | tf_op jit(solution)/shard_map/all_to_all | solution.py:197
  80.4 1.4 %fusion.48 = bf16[1024,256]{1,0:T(8,128)(2,1)S(1)} fusion(bf16[1024,256]{1,0:T(8,128)(2,1)} %get-tuple-element.32, bf16[1,2,1024,256]{3,2,1,0:T(8,128)(2,1)S(1)} %shard_map.86, bf16[32,8,2,128]{3,1,2,0:T(8,128)(2,1)S(1)} %get-tuple-element.42), kind=kOutput, calls=%fused_computation.88 | convolution fusion | flops 135528448 | bytes 1703936 | tf_op jit(solution)/shard_map/dot_general | solution.py:213
  81.8 1.4 %fusion.65 = bf16[256,256]{1,0:T(8,128)(2,1)S(1)} fusion(bf16[1024,256]{1,0:T(8,128)(2,1)S(1)} %fusion.48, bf16[1024,256]{1,0:T(8,128)(2,1)} %get-tuple-element.32, bf16[32,8,2,128]{3,1,2,0:T(8,128)(2,1)S(1)} %get-tuple-element.42), kind=kOutput, calls=%fused_computation.109 | convolution fusion | flops 134610944 | bytes 1310720 | tf_op jit(solution)/shard_map/dot_general | solution.py:221
  83.3 0.3 fusion.49
  83.6 0.3 fusion.64.token
  84.3 1.9 %collective-permute-start.6 = (bf16[256,256]{1,0:T(8,128)(2,1)S(1)}, bf16[256,256]{1,0:T(8,128)(2,1)S(1)}, u32[]{:S(2)}, u32[]{:S(2)}) collective-permute-start(bf16[256,256]{1,0:T(8,128)(2,1)S(1)} %fusion.65), channel_id=1, source_target_pairs={{0,127},{1,2},{2,1},{3,4},{4,3},{5,6},{6,5},{7,8},{8,7},{9,10},{10... | collective-permute-start | bytes 393224 | tf_op jit(solution)/shard_map/ppermute | solution.py:188
  86.1 1.2 collective-permute-start.7
  87.3 0.4 fusion.123
  87.7 4.0 %shard_map.87 = bf16[3,2,1024,256]{3,2,1,0:T(8,128)(2,1)S(1)} custom-call(s32[8,1024,512]{2,1,0:T(8,128)} %rated.9, bf16[8,1024,512]{2,1,0:T(8,128)(2,1)} %ratings.9, bf16[256,256]{1,0:T(8,128)(2,1)S(1)} %fusion.64.token), custom_call_target="tpu_custom_call" | custom-call | flops 1572864 | bytes 12582912 | tf_op jit(solution)/shard_map/pallas_call | solution.py:62
  91.6 4.4 %collective-permute-done.6 = bf16[256,256]{1,0:T(8,128)(2,1)S(1)} collective-permute-done((bf16[256,256]{1,0:T(8,128)(2,1)S(1)}, bf16[256,256]{1,0:T(8,128)(2,1)S(1)}, u32[]{:S(2)}, u32[]{:S(2)}) %collective-permute-start.6) | collective-permute-done | bytes 131104 | tf_op jit(solution)/shard_map/ppermute | solution.py:188
  96.4 0.4 fusion.88
  96.8 0.3 fusion.51
  97.2 0.4 fusion.94
  97.5 3.7 %collective-permute-start.9 = (bf16[256,256]{1,0:T(8,128)(2,1)S(1)}, bf16[256,256]{1,0:T(8,128)(2,1)S(1)}, u32[]{:S(2)}, u32[]{:S(2)}) collective-permute-start(bf16[256,256]{1,0:T(8,128)(2,1)S(1)} %fusion.94), channel_id=1, source_target_pairs={{0,127},{1,2},{2,1},{3,4},{4,3},{5,6},{6,5},{7,8},{8,7},{9,10},{10... | collective-permute-start | bytes 393224 | tf_op jit(solution)/shard_map/ppermute | solution.py:188
  101.5 0.4 fusion.124
  101.9 4.0 %collective-permute-done.8 = bf16[256,256]{1,0:T(8,128)(2,1)S(1)} collective-permute-done((bf16[256,256]{1,0:T(8,128)(2,1)S(1)}, bf16[256,256]{1,0:T(8,128)(2,1)S(1)}, u32[]{:S(2)}, u32[]{:S(2)}) %collective-permute-start.8) | collective-permute-done | bytes 131104 | tf_op jit(solution)/shard_map/ppermute | solution.py:182
  106.3 0.4 fusion.91
  106.7 1.8 %collective-permute-done.9 = bf16[256,256]{1,0:T(8,128)(2,1)S(1)} collective-permute-done((bf16[256,256]{1,0:T(8,128)(2,1)S(1)}, bf16[256,256]{1,0:T(8,128)(2,1)S(1)}, u32[]{:S(2)}, u32[]{:S(2)}) %collective-permute-start.9) | collective-permute-done | bytes 131104 | tf_op jit(solution)/shard_map/ppermute | solution.py:188
  108.5 0.3 fusion.53
  108.8 0.3 fusion.100
  109.6 0.4 fusion.125
  110.0 8.3 %collective-permute-done.10 = bf16[256,256]{1,0:T(8,128)(2,1)S(1)} collective-permute-done((bf16[256,256]{1,0:T(8,128)(2,1)S(1)}, bf16[256,256]{1,0:T(8,128)(2,1)S(1)}, u32[]{:S(2)}, u32[]{:S(2)}) %collective-permute-start.10) | collective-permute-done | bytes 131104 | tf_op jit(solution)/shard_map/ppermute | solution.py:188
  118.6 0.4 fusion.97
  118.9 0.3 fusion.55
  119.3 0.3 fusion.132
  119.9 0.8 broadcast_select_fusion
  120.7 1.3 %fusion.3 = f32[1024,256]{1,0:T(8,128)} fusion(f32[1024,256]{1,0:T(8,128)S(1)} %get-tuple-element.56, f32[1024,256]{1,0:T(8,128)S(1)} %fusion.131, bf16[1024,256]{1,0:T(8,128)(2,1)S(1)} %fusion.54, bf16[256,256]{1,0:T(8,128)(2,1)S(1)} %collective-permute-done.10), kind=kOutput, calls=%fused_computation.5 | convolution fusion | flops 135528448 | bytes 3801088 | tf_op jit(solution)/shard_map/dot_general | solution.py:229
  (34 shorter events, 3.9 us)
Async XLA Ops:
  3.3 16.9 %collective-permute-start = (bf16[256,256]{1,0:T(8,128)(2,1)S(1)}, bf16[256,256]{1,0:T(8,128)(2,1)S(1)}, u32[]{:S(2)}, u32[]{:S(2)}) collective-permute-start(bf16[256,256]{1,0:T(8,128)(2,1)S(1)} %fusion.67.token), channel_id=1, source_target_pairs={{0,127},{1,2},{2,1},{3,4},{4,3},{5,6},{6,5},{7,8},{8,7},{9,10},{10... | collective-permute-start | bytes 393224 | tf_op jit(solution)/shard_map/ppermute | solution.py:188
  15.5 8.4 %collective-permute-start.1 = (bf16[256,256]{1,0:T(8,128)(2,1)S(1)}, bf16[256,256]{1,0:T(8,128)(2,1)S(1)}, u32[]{:S(2)}, u32[]{:S(2)}) collective-permute-start(bf16[256,256]{1,0:T(8,128)(2,1)S(1)} %fusion.66.token), channel_id=1, source_target_pairs={{0,1},{1,0},{2,3},{3,2},{4,5},{5,4},{6,7},{7,6},{8,9},{9,8},{10,11... | collective-permute-start | bytes 393224 | tf_op jit(solution)/shard_map/ppermute | solution.py:182
  20.9 8.6 %collective-permute-start.2 = (bf16[256,256]{1,0:T(8,128)(2,1)S(1)}, bf16[256,256]{1,0:T(8,128)(2,1)S(1)}, u32[]{:S(2)}, u32[]{:S(2)}) collective-permute-start(bf16[256,256]{1,0:T(8,128)(2,1)S(1)} %fusion.70), channel_id=1, source_target_pairs={{0,1},{1,0},{2,3},{3,2},{4,5},{5,4},{6,7},{7,6},{8,9},{9,8},{10,11... | collective-permute-start | bytes 393224 | tf_op jit(solution)/shard_map/ppermute | solution.py:182
  24.7 10.9 %collective-permute-start.3 = (bf16[256,256]{1,0:T(8,128)(2,1)S(1)}, bf16[256,256]{1,0:T(8,128)(2,1)S(1)}, u32[]{:S(2)}, u32[]{:S(2)}) collective-permute-start(bf16[256,256]{1,0:T(8,128)(2,1)S(1)} %fusion.76), channel_id=1, source_target_pairs={{0,127},{1,2},{2,1},{3,4},{4,3},{5,6},{6,5},{7,8},{8,7},{9,10},{10... | collective-permute-start | bytes 393224 | tf_op jit(solution)/shard_map/ppermute | solution.py:188
  30.2 11.4 %collective-permute-start.4 = (bf16[256,256]{1,0:T(8,128)(2,1)S(1)}, bf16[256,256]{1,0:T(8,128)(2,1)S(1)}, u32[]{:S(2)}, u32[]{:S(2)}) collective-permute-start(bf16[256,256]{1,0:T(8,128)(2,1)S(1)} %fusion.73), channel_id=1, source_target_pairs={{0,127},{1,2},{2,1},{3,4},{4,3},{5,6},{6,5},{7,8},{8,7},{9,10},{10... | collective-permute-start | bytes 393224 | tf_op jit(solution)/shard_map/ppermute | solution.py:188
  36.3 6.0 %collective-permute-start.5 = (bf16[256,256]{1,0:T(8,128)(2,1)S(1)}, bf16[256,256]{1,0:T(8,128)(2,1)S(1)}, u32[]{:S(2)}, u32[]{:S(2)}) collective-permute-start(bf16[256,256]{1,0:T(8,128)(2,1)S(1)} %fusion.82), channel_id=1, source_target_pairs={{0,1},{1,0},{2,3},{3,2},{4,5},{5,4},{6,7},{7,6},{8,9},{9,8},{10,11... | collective-permute-start | bytes 393224 | tf_op jit(solution)/shard_map/ppermute | solution.py:182
  41.9 0.8 copy-start.2
  42.7 2.7 %copy-start.5 = (bf16[256,256]{1,0:T(8,128)(2,1)}, bf16[256,256]{1,0:T(8,128)(2,1)S(1)}, u32[]{:S(2)}) copy-start(bf16[256,256]{1,0:T(8,128)(2,1)S(1)} %collective-permute-done.5) | copy-start | bytes 393220
  43.1 2.4 %copy-start.4 = (bf16[1024,256]{1,0:T(8,128)(2,1)}, bf16[1024,256]{1,0:T(8,128)(2,1)S(1)}, u32[]{:S(2)}) copy-start(bf16[1024,256]{1,0:T(8,128)(2,1)S(1)} %fusion.47) | copy-start | bytes 1572868
  43.5 19.7 %copy-start = (s32[2,128]{1,0:T(2,128)S(1)}, s32[2,128]{1,0:T(2,128)}, u32[]{:S(2)}) copy-start(s32[2,128]{1,0:T(2,128)} %owners.1) | copy-start | bytes 3076
  46.2 17.0 %all-to-all-start = ((bf16[128,8,128]{2,1,0:T(8,128)(2,1)}), bf16[128,8,128]{2,1,0:T(8,128)(2,1)S(1)}, u32[]{:S(2)}, u32[]{:S(2)}) async-start(bf16[128,8,128]{2,1,0:T(8,128)(2,1)} %bitcast.17), calls=%async_computation | async-start | bytes 524288 | tf_op jit(solution)/shard_map/all_to_all | solution.py:197
  64.9 15.5 %all-to-all-start.1 = ((bf16[128,8,128]{2,1,0:T(8,128)(2,1)}), bf16[128,8,128]{2,1,0:T(8,128)(2,1)S(1)}, u32[]{:S(2)}, u32[]{:S(2)}) async-start(bf16[128,8,128]{2,1,0:T(8,128)(2,1)} %place.1), calls=%async_computation.1 | async-start | bytes 524288 | tf_op jit(solution)/shard_map/all_to_all | solution.py:197
  71.8 11.4 %copy-start.3 = (bf16[1024,256]{1,0:T(8,128)(2,1)S(1)}, bf16[1024,256]{1,0:T(8,128)(2,1)}, u32[]{:S(2)}) copy-start(bf16[1024,256]{1,0:T(8,128)(2,1)} %get-tuple-element.32) | copy-start | bytes 1572868
  83.2 4.1 %copy-start.1 = (f32[1024,256]{1,0:T(8,128)S(1)}, f32[1024,256]{1,0:T(8,128)}, u32[]{:S(2)}) copy-start(f32[1024,256]{1,0:T(8,128)} %get-tuple-element.50) | copy-start | bytes 3145732
  84.3 11.8 %collective-permute-start.6 = (bf16[256,256]{1,0:T(8,128)(2,1)S(1)}, bf16[256,256]{1,0:T(8,128)(2,1)S(1)}, u32[]{:S(2)}, u32[]{:S(2)}) collective-permute-start(bf16[256,256]{1,0:T(8,128)(2,1)S(1)} %fusion.65), channel_id=1, source_target_pairs={{0,127},{1,2},{2,1},{3,4},{4,3},{5,6},{6,5},{7,8},{8,7},{9,10},{10... | collective-permute-start | bytes 393224 | tf_op jit(solution)/shard_map/ppermute | solution.py:188
  86.1 10.7 %collective-permute-start.7 = (bf16[256,256]{1,0:T(8,128)(2,1)S(1)}, bf16[256,256]{1,0:T(8,128)(2,1)S(1)}, u32[]{:S(2)}, u32[]{:S(2)}) collective-permute-start(bf16[256,256]{1,0:T(8,128)(2,1)S(1)} %fusion.64.token), channel_id=1, source_target_pairs={{0,1},{1,0},{2,3},{3,2},{4,5},{5,4},{6,7},{7,6},{8,9},{9,8},{10,11... | collective-permute-start | bytes 393224 | tf_op jit(solution)/shard_map/ppermute | solution.py:182
  96.7 9.2 %collective-permute-start.8 = (bf16[256,256]{1,0:T(8,128)(2,1)S(1)}, bf16[256,256]{1,0:T(8,128)(2,1)S(1)}, u32[]{:S(2)}, u32[]{:S(2)}) collective-permute-start(bf16[256,256]{1,0:T(8,128)(2,1)S(1)} %fusion.88), channel_id=1, source_target_pairs={{0,1},{1,0},{2,3},{3,2},{4,5},{5,4},{6,7},{7,6},{8,9},{9,8},{10,11... | collective-permute-start | bytes 393224 | tf_op jit(solution)/shard_map/ppermute | solution.py:182
  97.5 10.9 %collective-permute-start.9 = (bf16[256,256]{1,0:T(8,128)(2,1)S(1)}, bf16[256,256]{1,0:T(8,128)(2,1)S(1)}, u32[]{:S(2)}, u32[]{:S(2)}) collective-permute-start(bf16[256,256]{1,0:T(8,128)(2,1)S(1)} %fusion.94), channel_id=1, source_target_pairs={{0,127},{1,2},{2,1},{3,4},{4,3},{5,6},{6,5},{7,8},{8,7},{9,10},{10... | collective-permute-start | bytes 393224 | tf_op jit(solution)/shard_map/ppermute | solution.py:188
  106.6 11.6 %collective-permute-start.10 = (bf16[256,256]{1,0:T(8,128)(2,1)S(1)}, bf16[256,256]{1,0:T(8,128)(2,1)S(1)}, u32[]{:S(2)}, u32[]{:S(2)}) collective-permute-start(bf16[256,256]{1,0:T(8,128)(2,1)S(1)} %fusion.91), channel_id=1, source_target_pairs={{0,127},{1,2},{2,1},{3,4},{4,3},{5,6},{6,5},{7,8},{8,7},{9,10},{10... | collective-permute-start | bytes 393224 | tf_op jit(solution)/shard_map/ppermute | solution.py:188
  109.2 9.7 %collective-permute-start.11 = (bf16[256,256]{1,0:T(8,128)(2,1)S(1)}, bf16[256,256]{1,0:T(8,128)(2,1)S(1)}, u32[]{:S(2)}, u32[]{:S(2)}) collective-permute-start(bf16[256,256]{1,0:T(8,128)(2,1)S(1)} %fusion.100), channel_id=1, source_target_pairs={{0,1},{1,0},{2,3},{3,2},{4,5},{5,4},{6,7},{7,6},{8,9},{9,8},{10,11... | collective-permute-start | bytes 393224 | tf_op jit(solution)/shard_map/ppermute | solution.py:182
